TPU v7x, 32 devices: a whole 2x2x4 slice. The times are simulated.
32 devices in a mesh: group: 2 (over core), ctx: 8 (over z, x), mp: 2 (over y).
Axes of the slice: x: 2, y: 2, z: 4, core: 2. Of those that a mesh axis runs over, the one named last changes fastest.
Arguments:
- token_ids: int32 [2, 1024], P('group', 'ctx'), may hold values from 0 to 127
- span_offset: int32 [1], replicated, may hold values from 0 to 3071
- shard_lengths: int32 [8], P('ctx'), may hold values from 1 to 384
- embed_table: bfloat16 [128, 2560], P(None, 'mp'), may hold values from -6 to 6
- norm_gain: bfloat16 [2560], P('mp'), may hold values from 0.25 to 1.75
- query_weight: bfloat16 [2560, 2560], P('mp'), may hold values from -0.25 to 0.25
- key_weight: bfloat16 [2560, 2560], P('mp'), may hold values from -0.25 to 0.25
- value_weight: bfloat16 [2560, 2560], P('mp'), may hold values from -0.125 to 0.125
- cache_keys: bfloat16 [3072, 2560], P('ctx', 'mp'), may hold values from -440 to 440
- cache_values: bfloat16 [3072, 2560], P('ctx', 'mp'), may hold values from -6 to 6
Outputs:
- attended: bfloat16 [2, 1024, 2560], P('group', 'ctx', 'mp')
All inputs are finite; a program needn't handle non-finite values.
Results may differ from a plain program's by a relative error of at most 0.012.
The roundings to bfloat16 on the way count: a program that leaves them out, or rounds other values in their place, can miss the bound.
Values may be sent and summed in bfloat16 or wider, within the bound.
A program may use at most 256 MiB of HBM per device.

v0:
```python
import math

import jax
import jax.numpy as jnp
from jax import lax
from jax.sharding import PartitionSpec as P

D = 2560
HD = 80
PROT = 256
STEPS = 4


def passed_along(value, axis, steps):
    count = lax.axis_size(axis)
    first, last = (max(0, -steps), min(count, count - steps))
    return lax.ppermute(value, axis, [(source, source + steps) for source in range(first, last)])


def rotate(values_in, positions):
    row_count = values_in.shape[0]
    head_count = values_in.shape[1] // HD
    quarter = HD // 4
    column = (positions % PROT).astype(jnp.float32)
    homolog = (positions // PROT).astype(jnp.float32)
    frequency = 10000.0 ** (-jnp.arange(quarter, dtype=jnp.float32) / quarter)
    angles = jnp.stack([column[:, None] * frequency, homolog[:, None] * frequency], 1)
    cosine = jnp.cos(angles)[:, None, :, None, :]
    sine_table = jnp.sin(angles)[:, None, :, None, :]
    pieces = values_in.reshape(row_count, head_count, 2, 2, quarter)
    partner = jnp.stack([-pieces[:, :, :, 1], pieces[:, :, :, 0]], 3)
    return (pieces * cosine + partner * sine_table).reshape(row_count, head_count * HD)


def block_partial(
    query_block, start, all_keys, all_values, live_length, span_base, cache_count, decoding
):
    block_rows = query_block.shape[0]
    head_count = query_block.shape[1] // HD
    key_slots = all_keys.shape[0]
    query_heads = query_block.reshape(block_rows, head_count, HD)
    key_heads = all_keys.reshape(key_slots, head_count, HD)
    value_heads = all_values.reshape(key_slots, head_count, HD)
    scores = jnp.einsum(
        "qhd,khd->hqk", query_heads, key_heads, preferred_element_type=jnp.float32
    ) * (1.0 / math.sqrt(HD))
    slot = jnp.arange(key_slots, dtype=jnp.int32)
    query_index = start + jnp.arange(block_rows, dtype=jnp.int32)
    cache_live = (slot < cache_count) & (slot < live_length)
    span_index = span_base + slot - cache_count
    span_seen = (slot >= cache_count)[None, :] & (
        decoding | (span_index[None, :] <= query_index[:, None])
    )
    visible = (cache_live[None, :] | span_seen)[None]
    block_max = jnp.max(jnp.where(visible, scores, -1e30), -1)
    weights = jnp.where(visible, jnp.exp(scores - block_max[..., None]), 0.0)
    block_sum = jnp.sum(weights, -1)
    block_acc = jnp.einsum(
        "hqk,khd->qhd",
        weights.astype(jnp.bfloat16),
        value_heads,
        preferred_element_type=jnp.float32,
    )
    return (block_max.T, block_sum.T, block_acc.reshape(block_rows, head_count * HD))


def local(
    token_ids,
    span_offset,
    shard_lengths,
    embed_table,
    norm_gain,
    query_weight,
    key_weight,
    value_weight,
    cache_keys,
    cache_values,
):
    token_row = token_ids[0]
    row_count = token_row.shape[0]
    ctx_count = lax.axis_size("ctx")
    ctx_index = lax.axis_index("ctx")
    decoding = lax.axis_index("group") == 1
    one_hot = (
        token_row[:, None] == jnp.arange(embed_table.shape[0], dtype=jnp.int32)[None, :]
    ).astype(jnp.bfloat16)
    embedded = jnp.dot(one_hot, embed_table, preferred_element_type=jnp.float32)
    square_sum = lax.psum(jnp.sum(embedded * embedded, 1), "mp")
    normal_rows = (
        embedded * lax.rsqrt(square_sum / D + 1e-05)[:, None] * norm_gain.astype(jnp.float32)
    ).astype(jnp.bfloat16)
    query_part = jnp.dot(normal_rows, query_weight, preferred_element_type=jnp.float32)
    key_part = jnp.dot(normal_rows, key_weight, preferred_element_type=jnp.float32)
    value_part = jnp.dot(normal_rows, value_weight, preferred_element_type=jnp.float32)
    query_full, key_full, value_full = (
        lax.psum_scatter(query_part, "mp", scatter_dimension=1, tiled=True),
        lax.psum_scatter(key_part, "mp", scatter_dimension=1, tiled=True),
        lax.psum_scatter(value_part, "mp", scatter_dimension=1, tiled=True),
    )
    offset_value = span_offset[0]
    local_iota = jnp.arange(row_count, dtype=jnp.int32)
    positions = jnp.where(
        decoding,
        offset_value + row_count * ctx_count + local_iota % STEPS,
        offset_value + ctx_index * row_count + local_iota,
    )
    queries = rotate(query_full, positions).astype(jnp.bfloat16)
    new_keys = rotate(key_full, positions).astype(jnp.bfloat16)
    new_values = value_full.astype(jnp.bfloat16)
    width = queries.shape[1]
    head_count = width // HD
    span_keys, span_values = passed_along((new_keys, new_values), "group", 1)
    block_keys = jnp.where(decoding, span_keys, new_keys)
    block_values = jnp.where(decoding, span_values, new_values)
    cache_count = cache_keys.shape[0]
    all_keys = jnp.concatenate([cache_keys, block_keys], 0)
    all_values = jnp.concatenate([cache_values, block_values], 0)
    live_length = shard_lengths[0]
    span_base = ctx_index * row_count
    gathered = lax.all_gather(queries, "ctx", axis=0, tiled=True)
    total = gathered.shape[0]
    block_rows = math.gcd(total, 512)
    block_count = total // block_rows
    block_starts = jnp.arange(block_count, dtype=jnp.int32) * block_rows

    def one_block(pair):
        return block_partial(
            pair[0], pair[1], all_keys, all_values, live_length, span_base, cache_count, decoding
        )

    maxima, totals, sums = lax.map(
        one_block, (gathered.reshape(block_count, block_rows, width), block_starts)
    )
    maxima = maxima.reshape(total, head_count)
    totals = totals.reshape(total, head_count)
    sums = sums.reshape(total, width)
    got_max, got_sum, got_acc = (
        lax.all_to_all(maxima[None], "ctx", split_axis=1, concat_axis=0, tiled=True),
        lax.all_to_all(totals[None], "ctx", split_axis=1, concat_axis=0, tiled=True),
        lax.all_to_all(sums[None], "ctx", split_axis=1, concat_axis=0, tiled=True),
    )
    whole_max = jnp.max(got_max, 0)
    rescale = jnp.exp(got_max - whole_max[None])
    whole_sum = jnp.sum(rescale * got_sum, 0)
    whole_acc = jnp.sum(got_acc * jnp.repeat(rescale, HD, axis=2), 0)
    cands = row_count // STEPS
    own_q = queries.reshape(cands, STEPS, head_count, HD)
    own_k = new_keys.reshape(cands, STEPS, head_count, HD)
    own_v = new_values.reshape(cands, STEPS, head_count, HD)
    own_scores = jnp.einsum("ashd,athd->ahst", own_q, own_k, preferred_element_type=jnp.float32) * (
        1.0 / math.sqrt(HD)
    )
    step_iota = jnp.arange(STEPS, dtype=jnp.int32)
    own_visible = (step_iota[None, :] <= step_iota[:, None]) & decoding
    own_max = jnp.max(jnp.where(own_visible, own_scores, -1e30), -1)
    final_max = jnp.maximum(whole_max, own_max.transpose(0, 2, 1).reshape(row_count, head_count))
    keep_old = jnp.exp(whole_max - final_max)
    final_cand = final_max.reshape(cands, STEPS, head_count).transpose(0, 2, 1)
    own_weights = jnp.where(own_visible, jnp.exp(own_scores - final_cand[..., None]), 0.0)
    own_sum = jnp.sum(own_weights, -1).transpose(0, 2, 1).reshape(row_count, head_count)
    own_acc = jnp.einsum(
        "ahst,athd->ashd",
        own_weights.astype(jnp.bfloat16),
        own_v,
        preferred_element_type=jnp.float32,
    ).reshape(row_count, width)
    numer = whole_acc * jnp.repeat(keep_old, HD, axis=1) + own_acc
    denom = whole_sum * keep_old + own_sum
    output = numer / jnp.repeat(denom, HD, axis=1)
    return output.astype(jnp.bfloat16)[None]


def solution(mesh):
    placed = (
        P("group", "ctx"),
        P(),
        P("ctx"),
        P(None, "mp"),
        P("mp"),
        P("mp", None),
        P("mp", None),
        P("mp", None),
        P("ctx", "mp"),
        P("ctx", "mp"),
    )
    return jax.shard_map(
        local, mesh=mesh, in_specs=placed, out_specs=P("group", "ctx", "mp"), check_vma=False
    )
```

profile of v0, /device:TPU:0, one launch (start us, length us, event | category | flops | bytes accessed | tf_op | source)
XLA Modules:
  0.0 382.4 jit_solution(8588172545605878299)
XLA Ops:
  6.5 0.7 convert_element_type.51
  7.5 1.0 multiply_reduce_fusion.1
  8.5 5.9 %psum.7 = f32[128]{0:T(128)S(1)} all-reduce(f32[128]{0:T(128)S(1)} %get-tuple-element.257), channel_id=1, replica_groups=mesh['group'=2,'ctx'=8,'mp'=2] {'mp'}, use_global_device_ids=true, to_apply=%region_1.0 | all-reduce | flops 128 | bytes 1024 | tf_op jit(solution)/shard_map/psum | solution.py:88
  14.6 5.0 %fusion.29 = f32[128,2560]{1,0:T(8,128)} fusion(bf16[128,1280]{1,0:T(8,128)(2,1)S(1)} %multiply_convert_fusion, bf16[1280,2560]{1,0:T(8,128)(2,1)} %param.18), kind=kOutput, calls=%fused_computation.76 | convolution fusion | flops 838860800 | bytes 8192000 | tf_op jit(solution)/shard_map/dot_general | solution.py:93
  19.6 5.0 %fusion.28 = f32[128,2560]{1,0:T(8,128)} fusion(bf16[128,1280]{1,0:T(8,128)(2,1)S(1)} %multiply_convert_fusion, bf16[1280,2560]{1,0:T(8,128)(2,1)} %param.17), kind=kOutput, calls=%fused_computation.75 | convolution fusion | flops 838860800 | bytes 8192000 | tf_op jit(solution)/shard_map/dot_general | solution.py:92
  24.7 5.0 %fusion.30 = f32[128,2560]{1,0:T(8,128)} fusion(bf16[128,1280]{1,0:T(8,128)(2,1)S(1)} %multiply_convert_fusion, bf16[1280,2560]{1,0:T(8,128)(2,1)} %param.19), kind=kOutput, calls=%fused_computation.77 | convolution fusion | flops 838860800 | bytes 8192000 | tf_op jit(solution)/shard_map/dot_general | solution.py:94
  30.8 1.1 copy.156
  31.9 12.9 %reduce-scatter.6.cloned.1.call-done = f32[128,1280]{1,0:T(8,128)} async-done(((f32[128,2560]{1,0:T(8,128)}), f32[128,1280]{1,0:T(8,128)}) %reduce-scatter.6.cloned.1.call-update) | async-done | bytes 655376 | tf_op jit(solution)/shard_map/reduce_scatter | solution.py:97
  44.8 1.3 copy.160
  46.2 24.2 %reduce-scatter.4.cloned.1.call-done = f32[128,1280]{1,0:T(8,128)} async-done(((f32[128,2560]{1,0:T(8,128)}), f32[128,1280]{1,0:T(8,128)}) %reduce-scatter.4.cloned.1.call-update) | async-done | bytes 655376 | tf_op jit(solution)/shard_map/reduce_scatter | solution.py:96
  70.3 1.3 copy.157
  72.0 1.1 copy.158
  73.4 2.6 add_convert_fusion.1
  76.0 1.6 collective-permute-start
  77.7 1.7 copy.162
  79.4 1.6 copy.164
  81.0 14.9 %reduce-scatter.8.cloned.1.call-done = f32[128,1280]{1,0:T(8,128)} async-done(((f32[128,2560]{1,0:T(8,128)}), f32[128,1280]{1,0:T(8,128)}) %reduce-scatter.8.cloned.1.call-update) | async-done | bytes 655376 | tf_op jit(solution)/shard_map/reduce_scatter | solution.py:98
  95.9 1.1 convert_element_type.57
  97.0 2.3 collective-permute-start.1
  100.0 1.9 broadcast_select_fusion
  101.8 1.2 copy.165
  103.0 1.2 pad_maximum_fusion
  104.2 1.2 pad_maximum_fusion.1
  105.4 46.9 %all-gather.2.cloned.1.call-done = bf16[1024,1280]{1,0:T(8,128)(2,1)} async-done(((bf16[128,1280]{1,0:T(8,128)(2,1)}), bf16[1024,1280]{1,0:T(8,128)(2,1)}) %all-gather.2.cloned.1.call-update) | async-done | bytes 2621456 | tf_op jit(solution)/shard_map/all_gather | solution.py:120
  152.3 70.8 %while.16 = (s32[]{:T(128)}, f32[2,512,16]{1,2,0:T(8,128)S(1)}, f32[2,512,16]{1,2,0:T(8,128)S(1)}, f32[2,512,1280]{2,1,0:T(8,128)}, s32[]{:T(128)}, /*index=5*/p...) while((s32[]{:T(128)}, f32[2,512,16]{1,2,0:T(8,128)S(1)}, ...), condition=%wide.region_8.9_spmd, body=%wide.region_5.8_spmd.sunk | while | flops 1389350400 | bytes 79177912 | solution.py:131
  154.6 1.4 constant_dynamic-slice_fusion.2
  156.7 8.8 %select_reduce_fusion.3 = (f32[16,512]{1,0:T(8,128)S(1)}, f32[16,512,512]{1,2,0:T(8,128)}) fusion(pred[512,512]{0,1:T(8,128)(4,1)S(1)} %and_or_fusion.2, bf16[512,16,80]{0,2,1:T(8,128)(2,1)S(1)} %bitcast.97, bf16[512,16,80]{0,2,1:T(8,128)(2,1)} %bitcast.99), kind=kOutput, calls=%fused_computation.1.clone.1 | convolution fusion | flops 683663360 | bytes 19693568 | tf_op jit(solution)/shard_map/while/body/eval_jaxpr/qhd,khd->hqk/dot_general | solution.py:44
  165.5 9.3 %fusion.54 = f32[16,512]{1,0:T(8,128)S(1)} fusion(f32[16,512,512]{1,2,0:T(8,128)} %get-tuple-element.334, f32[16,512]{1,0:T(8,128)S(1)} %get-tuple-element.335, pred[512,512]{0,1:T(8,128)(4,1)S(1)} %and_or_fusion.2), kind=kLoop, calls=%fused_computation.3.clone.1 | loop fusion | flops 16769024 | bytes 17104896 | tf_op jit(solution)/shard_map/while/body/eval_jaxpr/reduce_sum | solution.py:57
  174.7 9.2 %fusion.55 = f32[16,512,80]{1,2,0:T(8,128)} fusion(bf16[512,16,80]{0,2,1:T(8,128)(2,1)S(1)} %bitcast.111, f32[16,512,512]{1,2,0:T(8,128)} %get-tuple-element.334, f32[16,512]{1,0:T(8,128)S(1)} %get-tuple-element.335, pred[512,512]{0,1:T(8,128)(4,1)S(1)} %and_or_fusion.2), kind=kOutput, calls=%fused_computation.4.clone.1 | convolution fusion | flops 687865856 | bytes 21004288 | tf_op jit(solution)/shard_map/while/body/eval_jaxpr/hqk,khd->qhd/dot_general | solution.py:58
  183.9 2.1 copy.222
  186.1 1.7 constant_dynamic-update-slice_fusion.2
  190.0 1.4 constant_dynamic-slice_fusion.2
  192.1 8.8 %select_reduce_fusion.3 = (f32[16,512]{1,0:T(8,128)S(1)}, f32[16,512,512]{1,2,0:T(8,128)}) fusion(pred[512,512]{0,1:T(8,128)(4,1)S(1)} %and_or_fusion.2, bf16[512,16,80]{0,2,1:T(8,128)(2,1)S(1)} %bitcast.97, bf16[512,16,80]{0,2,1:T(8,128)(2,1)} %bitcast.99), kind=kOutput, calls=%fused_computation.1.clone.1 | convolution fusion | flops 683663360 | bytes 19693568 | tf_op jit(solution)/shard_map/while/body/eval_jaxpr/qhd,khd->hqk/dot_general | solution.py:44
  200.8 9.3 %fusion.54 = f32[16,512]{1,0:T(8,128)S(1)} fusion(f32[16,512,512]{1,2,0:T(8,128)} %get-tuple-element.334, f32[16,512]{1,0:T(8,128)S(1)} %get-tuple-element.335, pred[512,512]{0,1:T(8,128)(4,1)S(1)} %and_or_fusion.2), kind=kLoop, calls=%fused_computation.3.clone.1 | loop fusion | flops 16769024 | bytes 17104896 | tf_op jit(solution)/shard_map/while/body/eval_jaxpr/reduce_sum | solution.py:57
  210.1 9.2 %fusion.55 = f32[16,512,80]{1,2,0:T(8,128)} fusion(bf16[512,16,80]{0,2,1:T(8,128)(2,1)S(1)} %bitcast.111, f32[16,512,512]{1,2,0:T(8,128)} %get-tuple-element.334, f32[16,512]{1,0:T(8,128)S(1)} %get-tuple-element.335, pred[512,512]{0,1:T(8,128)(4,1)S(1)} %and_or_fusion.2), kind=kOutput, calls=%fused_computation.4.clone.1 | convolution fusion | flops 687865856 | bytes 21004288 | tf_op jit(solution)/shard_map/while/body/eval_jaxpr/hqk,khd->qhd/dot_general | solution.py:58
  219.3 2.1 copy.222
  221.4 1.7 constant_dynamic-update-slice_fusion.2
  223.9 2.0 reduce
  225.9 0.8 reshape.390
  226.7 3.6 all-to-all-start.1
  230.5 2.0 reduce.2
  232.5 0.9 reshape.392
  233.4 3.6 all-to-all-done.1
  236.9 3.3 all-to-all-start.2
  240.3 10.2 %copy.168 = f32[1,1024,1280]{2,0,1:T(1,128)} copy(f32[1,1024,1280]{2,1,0:T(8,128)} %bitcast.103) | data formatting | bytes 10485760 | tf_op jit(solution)/shard_map/broadcast_in_dim;reshape | solution.py:140
  250.5 6.1 %all-to-all-start = ((f32[1,1024,1280]{2,0,1:T(1,128)}), f32[1,1024,1280]{2,0,1:T(1,128)}, u32[]{:S(2)}, u32[]{:S(2)}) async-start(f32[1,1024,1280]{2,0,1:T(1,128)} %copy.168), calls=%async_computation.3 | async-start | bytes 10485760 | tf_op jit(solution)/shard_map/all_to_all | solution.py:140
  256.6 0.8 reshape.383
  257.4 0.8 reshape.382
  258.2 0.8 reshape.386
  259.0 0.7 fusion.12
  259.7 0.7 copy.177
  260.8 0.8 reduce.1
  261.7 0.9 reshape.391
  263.7 0.8 reduce.3
  264.5 0.9 reshape.393
  266.0 1.0 copy.186
  267.0 0.7 convolution_bitcast_fusion
  268.6 2.6 broadcast_in_dim.99
  271.2 5.9 %copy.174 = f32[8,128,1280]{2,1,0:T(8,128)} copy(f32[8,128,1280]{1,2,0:T(8,128)} %bitcast.101) | data formatting | bytes 10485760 | tf_op jit(solution)/shard_map/reshape | solution.py:145
  277.1 92.9 %all-to-all-done = f32[1,1024,1280]{2,0,1:T(1,128)} async-done(((f32[1,1024,1280]{2,0,1:T(1,128)}), f32[1,1024,1280]{2,0,1:T(1,128)}, u32[]{:S(2)}, u32[]{:S(2)}) %all-to-all-start) | async-done | bytes 5242912 | tf_op jit(solution)/shard_map/all_to_all | solution.py:140
  370.0 3.0 copy.203
  373.0 1.0 copy-done.2
  374.0 0.9 multiply_reduce_fusion
  374.9 0.9 fusion.10
  (90 shorter events, 11.8 us)
Async XLA Ops:
  6.5 1.0 copy-start
  6.5 38.2 %reduce-scatter.6.cloned.1.call-start = ((), (), s32[]{:S(2)}) async-start(), calls=%async_computation.8 | async-start | bytes 1966080 | tf_op jit(solution)/shard_map/reduce_scatter | solution.py:97
  19.6 50.7 %reduce-scatter.4.cloned.1.call-start = ((), (), s32[]{:S(2)}) async-start(), calls=%async_computation.6 | async-start | bytes 1966080 | tf_op jit(solution)/shard_map/reduce_scatter | solution.py:96
  24.6 71.3 %reduce-scatter.8.cloned.1.call-start = ((), (), s32[]{:S(2)}) async-start(), calls=%async_computation.9 | async-start | bytes 1966080 | tf_op jit(solution)/shard_map/reduce_scatter | solution.py:98
  29.7 122.6 %all-gather.2.cloned.1.call-start = ((), (), s32[]{:S(2)}) async-start(), calls=%async_computation.7 | async-start | bytes 2949120 | tf_op jit(solution)/shard_map/all_gather | solution.py:120
  76.0 23.3 %collective-permute-start = (bf16[128,1280]{1,0:T(8,128)(2,1)S(1)}, bf16[128,1280]{1,0:T(8,128)(2,1)S(1)}, u32[]{:S(2)}, u32[]{:S(2)}) collective-permute-start(bf16[128,1280]{1,0:T(8,128)(2,1)S(1)} %get-tuple-element.248), channel_id=1, source_target_pairs={{0,16},{1,17},{2,18},{3,19},{4,20},{5,21},{6,22},{7,23},{8,24},{9,... | collective-permute-start | bytes 983048 | tf_op jit(solution)/shard_map/ppermute | solution.py:17
  97.0 55.3 %copy-start.5 = (bf16[128,1280]{1,0:T(8,128)(2,1)}, bf16[128,1280]{1,0:T(8,128)(2,1)S(1)}, u32[]{:S(2)}) copy-start(bf16[128,1280]{1,0:T(8,128)(2,1)S(1)} %convert_element_type.57) | copy-start | bytes 983044
  97.0 2.9 collective-permute-start.1
  165.5 9.3 %copy-start.4 = (bf16[512,1280]{0,1:T(8,128)(2,1)S(1)}, bf16[512,1280]{0,1:T(8,128)(2,1)}, u32[]{:S(2)}) copy-start(bf16[512,1280]{0,1:T(8,128)(2,1)} %get-tuple-element.372) | copy-start | bytes 3932164 | tf_op jit(solution)/shard_map/while
  200.8 9.3 %copy-start.4 = (bf16[512,1280]{0,1:T(8,128)(2,1)S(1)}, bf16[512,1280]{0,1:T(8,128)(2,1)}, u32[]{:S(2)}) copy-start(bf16[512,1280]{0,1:T(8,128)(2,1)} %get-tuple-element.372) | copy-start | bytes 3932164 | tf_op jit(solution)/shard_map/while
  226.7 10.2 %all-to-all-start.1 = ((f32[8,1,2048]{2,1,0:T(1,128)}), f32[8,1,2048]{2,1,0:T(1,128)S(1)}, u32[]{:S(2)}, u32[]{:S(2)}) async-start(f32[8,1,2048]{2,1,0:T(1,128)} %reshape.390), calls=%async_computation.4 | async-start | bytes 131072 | tf_op jit(solution)/shard_map/all_to_all | solution.py:138
  236.9 13.6 %all-to-all-start.2 = ((f32[8,1,2048]{2,1,0:T(1,128)}), f32[8,1,2048]{2,1,0:T(1,128)S(1)}, u32[]{:S(2)}, u32[]{:S(2)}) async-start(f32[8,1,2048]{2,1,0:T(1,128)} %reshape.392), calls=%async_computation.5 | async-start | bytes 131072 | tf_op jit(solution)/shard_map/all_to_all | solution.py:139
  250.5 6.9 %copy-start.3 = (bf16[128,1280]{1,0:T(8,128)(2,1)S(1)}, bf16[128,1280]{1,0:T(8,128)(2,1)}, u32[]{:S(2)}) copy-start(bf16[128,1280]{1,0:T(8,128)(2,1)} %get-tuple-element.247) | copy-start | bytes 983044
  250.5 7.7 %copy-start.6 = (bf16[128,1280]{1,0:T(8,128)(2,1)S(1)}, bf16[128,1280]{1,0:T(8,128)(2,1)}, u32[]{:S(2)}) copy-start(bf16[128,1280]{1,0:T(8,128)(2,1)} %copy-done.5) | copy-start | bytes 983044
  250.5 119.5 %all-to-all-start = ((f32[1,1024,1280]{2,0,1:T(1,128)}), f32[1,1024,1280]{2,0,1:T(1,128)}, u32[]{:S(2)}, u32[]{:S(2)}) async-start(f32[1,1024,1280]{2,0,1:T(1,128)} %copy.168), calls=%async_computation.3 | async-start | bytes 10485760 | tf_op jit(solution)/shard_map/all_to_all | solution.py:140
  370.0 4.0 %copy-start.2 = (f32[8,128,1280]{2,1,0:T(8,128)S(1)}, f32[8,128,1280]{2,1,0:T(8,128)}, u32[]{:S(2)}) copy-start(f32[8,128,1280]{2,1,0:T(8,128)} %copy.174) | copy-start | bytes 15728644
  373.0 2.9 copy-start.1
Sparse Core Ops, SparseCore 0:
  19.7 25.0 reduce-scatter.5
  47.0 23.2 reduce-scatter.3
  72.6 23.2 reduce-scatter.7
  97.9 54.3 all-gather.1
where the time goes:
time: 384 us; the launch traced here: 382 us
  waiting for transfers between devices  196 us (51%)
  local copies, waits for them, and re-layouts  57.1 us (15%)
  matrix products  53.2 us (14%)
  other arithmetic  38.9 us (10%)
  starting transfers between devices  17 us (4%)
  between operations  14.2 us (4%)
  blocking collectives  5.9 us (2%)
    all_to_all x1, waiting for transfers between devices, local(): lax.all_to_all(sums[None], 'ctx', split_axis=1, concat_axis=0, tiled=True)  92.9 us
    all_gather x1, waiting for transfers between devices, local(): gathered = lax.all_gather(queries, 'ctx', axis=0, tiled=True)  46.9 us
    reduce_scatter x1, waiting for transfers between devices, local(): lax.psum_scatter(query_part, 'mp', scatter_dimension=1, tiled=True)  24.2 us
    reduce_sum x2, other arithmetic, block_partial(): block_sum = jnp.sum(weights, -1)  18.5 us
    dot_general x2, matrix products, block_partial(): jnp.einsum('hqk,khd->qhd', weights.astype(jnp.bfloat16), value_heads, pre...  18.3 us
    dot_general x2, matrix products, block_partial(): jnp.einsum('qhd,khd->hqk', query_heads, key_heads, preferred_element_type...  17.6 us
    reduce_scatter x1, waiting for transfers between devices, local(): lax.psum_scatter(value_part, 'mp', scatter_dimension=1, tiled=True)  14.9 us
    reduce_scatter x1, waiting for transfers between devices, local(): lax.psum_scatter(key_part, 'mp', scatter_dimension=1, tiled=True)  12.9 us
  transfers between devices with their start and end apart: 9, of which 7 were waited for; matrix products, arithmetic and copies ran while one was open for 16% of the time, Pallas kernels for 0%

commit v1 on v0

--- a/solution.py
+++ b/solution.py
@@ -3,6 +3,8 @@
 import jax
 import jax.numpy as jnp
 from jax import lax
+from jax.experimental import pallas as pl
+from jax.experimental.pallas import tpu as pltpu
 from jax.sharding import PartitionSpec as P
 
 D = 2560
@@ -170,6 +172,385 @@
     return output.astype(jnp.bfloat16)[None]
 
 
+MESH_ID = pl.DeviceIdType.MESH
+META = 16
+WINDOW = 256
+
+
+def exchange_kernel(
+    packed, embed, gain, wq, wk, wv, kv, table, wbuf, ss_out, ss_in, part_out, part_in, wsem, own_sem,
+    send_sem, recv_sem, relay_send, relay_recv, mp_send, mp_recv,
+):
+    count = packed.shape[0]
+    span = packed.shape[1] - META
+    group, ctx, mp = lax.axis_index("group"), lax.axis_index("ctx"), lax.axis_index("mp")
+    half = wq.shape[1] // 2
+    first = pl.multiple_of(ctx * span // 128 * 128, 128)
+    barrier = pltpu.get_barrier_semaphore()
+    for step in range(1, count):
+        pl.semaphore_signal(
+            barrier, inc=1, device_id={"ctx": lax.rem(ctx + step, count)}, device_id_type=MESH_ID
+        )
+    pl.semaphore_signal(barrier, inc=1, device_id={"group": 1 - group}, device_id_type=MESH_ID)
+    pl.semaphore_signal(barrier, inc=1, device_id={"mp": 1 - mp}, device_id_type=MESH_ID)
+    loads = []
+    for slot in range(6):
+        side = 1 - mp if slot < 3 else mp
+        weight = (wq, wk, wv)[slot % 3]
+        column = pl.multiple_of(side * half + first, 128)
+        loads.append(
+            pltpu.make_async_copy(
+                weight.at[:, pl.ds(column, WINDOW)], wbuf.at[slot], wsem.at[slot]
+            )
+        )
+        loads[-1].start()
+    mine = pltpu.make_async_copy(packed.at[ctx], kv.at[group, ctx], own_sem)
+    mine.start()
+    pl.semaphore_wait(barrier, count + 1)
+    sends = []
+    for step in range(1, count):
+        target = lax.rem(ctx + step, count)
+        sends.append(
+            pltpu.make_async_remote_copy(
+                src_ref=packed.at[target],
+                dst_ref=kv.at[group, ctx],
+                send_sem=send_sem.at[step],
+                recv_sem=recv_sem.at[step],
+                device_id={"ctx": target},
+                device_id_type=MESH_ID,
+            )
+        )
+        sends[-1].start()
+    relays = [
+        pltpu.make_async_remote_copy(
+            src_ref=packed.at[ctx],
+            dst_ref=kv.at[group, ctx],
+            send_sem=relay_send.at[0],
+            recv_sem=relay_recv.at[0],
+            device_id={"group": 1 - group},
+            device_id_type=MESH_ID,
+        )
+    ]
+    relays[0].start()
+    rows = embed[...].astype(jnp.float32)
+    ss_out[...] = jnp.broadcast_to(jnp.sum(rows * rows, 1, keepdims=True), ss_out.shape)
+    squares = pltpu.make_async_remote_copy(
+        src_ref=ss_out,
+        dst_ref=ss_in,
+        send_sem=mp_send.at[0],
+        recv_sem=mp_recv.at[0],
+        device_id={"mp": 1 - mp},
+        device_id_type=MESH_ID,
+    )
+    squares.start()
+    squares.wait()
+    square_sum = (ss_out[...] + ss_in[...])[:, :1]
+    normal = (
+        rows * lax.rsqrt(square_sum / D + 1e-05) * gain[...].astype(jnp.float32)
+    ).astype(jnp.bfloat16)
+    for slot in range(3):
+        loads[slot].wait()
+        part_out[slot] = jnp.dot(normal, wbuf[slot], preferred_element_type=jnp.float32)
+    parts = pltpu.make_async_remote_copy(
+        src_ref=part_out,
+        dst_ref=part_in,
+        send_sem=mp_send.at[1],
+        recv_sem=mp_recv.at[1],
+        device_id={"mp": 1 - mp},
+        device_id_type=MESH_ID,
+    )
+    parts.start()
+    for slot in range(3):
+        loads[slot + 3].wait()
+        table[slot] = jnp.dot(normal, wbuf[slot + 3], preferred_element_type=jnp.float32)
+    parts.wait()
+    shift = WINDOW - (ctx * span - first)
+    for slot in range(3):
+        table[slot] = pltpu.roll(table[slot] + part_in[slot], lax.rem(shift, WINDOW), 1)
+    for step in range(1, count):
+        source = lax.rem(ctx + count - step, count)
+        sends[step - 1].wait_recv()
+        relays.append(
+            pltpu.make_async_remote_copy(
+                src_ref=kv.at[group, source],
+                dst_ref=kv.at[group, source],
+                send_sem=relay_send.at[step],
+                recv_sem=relay_recv.at[step],
+                device_id={"group": 1 - group},
+                device_id_type=MESH_ID,
+            )
+        )
+        relays[-1].start()
+    mine.wait()
+    for step in range(1, count):
+        sends[step - 1].wait_send()
+    for relay in relays:
+        relay.wait()
+
+
+def exchange(packed, embed, gain, wq, wk, wv):
+    count = packed.shape[0]
+    vocab, features = embed.shape
+    vmem = pl.BlockSpec(memory_space=pltpu.VMEM)
+    anywhere = pl.BlockSpec(memory_space=pl.ANY)
+    return pl.pallas_call(
+        exchange_kernel,
+        out_shape=(
+            jax.ShapeDtypeStruct((2,) + packed.shape, jnp.bfloat16),
+            jax.ShapeDtypeStruct((3, vocab, WINDOW), jnp.float32),
+        ),
+        in_specs=[anywhere, vmem, vmem, anywhere, anywhere, anywhere],
+        out_specs=(anywhere, vmem),
+        scratch_shapes=[
+            pltpu.VMEM((6, features, WINDOW), jnp.bfloat16),
+            pltpu.VMEM((vocab, 128), jnp.float32),
+            pltpu.VMEM((vocab, 128), jnp.float32),
+            pltpu.VMEM((3, vocab, WINDOW), jnp.float32),
+            pltpu.VMEM((3, vocab, WINDOW), jnp.float32),
+            pltpu.SemaphoreType.DMA((6,)),
+            pltpu.SemaphoreType.DMA,
+            pltpu.SemaphoreType.DMA((count,)),
+            pltpu.SemaphoreType.DMA((count,)),
+            pltpu.SemaphoreType.DMA((count,)),
+            pltpu.SemaphoreType.DMA((count,)),
+            pltpu.SemaphoreType.DMA((2,)),
+            pltpu.SemaphoreType.DMA((2,)),
+        ],
+        compiler_params=pltpu.CompilerParams(collective_id=0, has_side_effects=True),
+        name="exchange",
+    )(packed, embed, gain, wq, wk, wv)
+
+
+def attention_kernel(query, own_key, own_value, span_key, span_value, kv, bias, out, scores):
+    row_block, width = query.shape
+    count, keep = kv.shape[1], kv.shape[3]
+    span_rows = span_key.shape[0]
+    start = pl.program_id(0) * row_block
+    decoding = lax.axis_index("group") == 1
+    scale = 1.0 / math.sqrt(HD)
+    across = (((1,), (1,)), ((), ()))
+    row = lax.broadcasted_iota(jnp.int32, (row_block, span_rows), 0) + start
+    col = lax.broadcasted_iota(jnp.int32, (row_block, span_rows), 1)
+    limit = jnp.where(decoding, span_rows, row)
+    own_row = lax.broadcasted_iota(jnp.int32, (row_block, row_block), 0)
+    own_col = lax.broadcasted_iota(jnp.int32, (row_block, row_block), 1)
+    own_limit = jnp.where(decoding, own_row, -1)
+    own_seen = (own_row // STEPS == own_col // STEPS) & (own_col <= own_limit)
+    lane = lax.broadcasted_iota(jnp.int32, (row_block, width), 1)
+    result = None
+    span_at = count * keep
+    own_at = span_at + span_rows
+    total = own_at + row_block
+    for head in range(width // HD):
+        inside = (lane >= head * HD) & (lane < (head + 1) * HD)
+        head_query = jnp.where(inside, query[...], jnp.zeros_like(query[...]))
+        for block in range(count):
+            part = jnp.dot(head_query, kv[0, block, :width, :], preferred_element_type=jnp.float32)
+            scores[:, block * keep : (block + 1) * keep] = part + bias[block]
+        part = lax.dot_general(
+            head_query, span_key[...], across, preferred_element_type=jnp.float32
+        )
+        scores[:, span_at:own_at] = jnp.where(col <= limit, part, -1e30)
+        part = lax.dot_general(
+            head_query, own_key[...], across, preferred_element_type=jnp.float32
+        )
+        scores[:, own_at:total] = jnp.where(own_seen, part, -1e30)
+        top = jnp.max(scores[...], 1, keepdims=True)
+        norm = jnp.zeros((row_block, 1), jnp.float32)
+        acc = jnp.zeros((row_block, width), jnp.float32)
+        for block in range(count):
+            weights = jnp.exp((scores[:, block * keep : (block + 1) * keep] - top) * scale)
+            norm += jnp.sum(weights, 1, keepdims=True)
+            acc += lax.dot_general(
+                weights.astype(jnp.bfloat16),
+                kv[1, block, :width, :],
+                across,
+                preferred_element_type=jnp.float32,
+            )
+        for at, end, values in ((span_at, own_at, span_value), (own_at, total, own_value)):
+            weights = jnp.exp((scores[:, at:end] - top) * scale)
+            norm += jnp.sum(weights, 1, keepdims=True)
+            acc += jnp.dot(
+                weights.astype(jnp.bfloat16), values[...], preferred_element_type=jnp.float32
+            )
+        head_out = acc / norm
+        result = head_out if result is None else jnp.where(inside, head_out, result)
+    padded = jnp.concatenate(
+        [result, jnp.zeros((row_block, -width % 128), jnp.float32)], 1
+    )
+    out[...] = jnp.transpose(padded)[:width].astype(jnp.bfloat16)[None]
+
+
+def attention(query, own_key, own_value, span_key, span_value, kv, bias, row_block):
+    rows, width = query.shape
+    span_rows = span_key.shape[0]
+    blocks = rows // row_block
+    keys = kv.shape[1] * kv.shape[3] + span_rows + row_block
+    by_rows = pl.BlockSpec((row_block, width), lambda i: (i, 0))
+    whole = pl.BlockSpec((span_rows, width), lambda i: (0, 0))
+    return pl.pallas_call(
+        attention_kernel,
+        grid=(blocks,),
+        out_shape=jax.ShapeDtypeStruct((blocks, width, row_block), jnp.bfloat16),
+        in_specs=[
+            by_rows,
+            by_rows,
+            by_rows,
+            whole,
+            whole,
+            pl.BlockSpec(kv.shape, lambda i: (0, 0, 0, 0)),
+            pl.BlockSpec(bias.shape, lambda i: (0, 0, 0)),
+        ],
+        out_specs=pl.BlockSpec((1, width, row_block), lambda i: (i, 0, 0)),
+        scratch_shapes=[pltpu.VMEM((row_block, keys), jnp.float32)],
+        compiler_params=pltpu.CompilerParams(vmem_limit_bytes=56 << 20),
+        name="attention",
+    )(query, own_key, own_value, span_key, span_value, kv, bias)
+
+
+def give_back_kernel(parts, got, own_sem, send_sem, recv_sem):
+    count = parts.shape[0]
+    ctx = lax.axis_index("ctx")
+    barrier = pltpu.get_barrier_semaphore()
+    for step in range(1, count):
+        pl.semaphore_signal(
+            barrier, inc=1, device_id={"ctx": lax.rem(ctx + step, count)}, device_id_type=MESH_ID
+        )
+    mine = pltpu.make_async_copy(parts.at[ctx], got.at[ctx], own_sem)
+    mine.start()
+    pl.semaphore_wait(barrier, count - 1)
+    sends = []
+    for step in range(1, count):
+        target = lax.rem(ctx + step, count)
+        sends.append(
+            pltpu.make_async_remote_copy(
+                src_ref=parts.at[target],
+                dst_ref=got.at[ctx],
+                send_sem=send_sem.at[step],
+                recv_sem=recv_sem.at[step],
+                device_id={"ctx": target},
+                device_id_type=MESH_ID,
+            )
+        )
+        sends[-1].start()
+    mine.wait()
+    for send in sends:
+        send.wait()
+
+
+def give_back(parts):
+    count = parts.shape[0]
+    anywhere = pl.BlockSpec(memory_space=pl.ANY)
+    return pl.pallas_call(
+        give_back_kernel,
+        out_shape=jax.ShapeDtypeStruct(parts.shape, parts.dtype),
+        in_specs=[anywhere],
+        out_specs=anywhere,
+        scratch_shapes=[
+            pltpu.SemaphoreType.DMA,
+            pltpu.SemaphoreType.DMA((count,)),
+            pltpu.SemaphoreType.DMA((count,)),
+        ],
+        compiler_params=pltpu.CompilerParams(collective_id=1, has_side_effects=True),
+        name="give_back",
+    )(parts)
+
+
+def split_three(values):
+    high = lax.reduce_precision(values, 8, 7)
+    rest = values - high
+    middle = lax.reduce_precision(rest, 8, 7)
+    return jnp.concatenate([high, middle, rest - middle], 0).astype(jnp.bfloat16)
+
+
+def partner(table):
+    pieces = table.reshape(table.shape[0], -1, 2, 2, HD // 4)
+    swapped = jnp.stack([-pieces[:, :, :, 1], pieces[:, :, :, 0]], 3)
+    return swapped.reshape(table.shape)
+
+
+def rotation(positions, width):
+    quarter = HD // 4
+    lane = jnp.arange(width) % HD
+    frequency = 10000.0 ** (-(lane % quarter).astype(jnp.float32) / quarter)
+    column = (positions % PROT).astype(jnp.float32)
+    homolog = (positions // PROT).astype(jnp.float32)
+    angles = jnp.where(lane[None] < HD // 2, column[:, None], homolog[:, None]) * frequency[None]
+    return jnp.cos(angles), jnp.sin(angles)
+
+
+def by_heads(
+    token_ids,
+    span_offset,
+    shard_lengths,
+    embed_table,
+    norm_gain,
+    query_weight,
+    key_weight,
+    value_weight,
+    cache_keys,
+    cache_values,
+):
+    row_count = token_ids.shape[1]
+    count = lax.axis_size("ctx")
+    rows = row_count * count
+    cache_count, local_width = cache_keys.shape
+    width = local_width // count
+    vocab = embed_table.shape[0]
+    decoding = lax.axis_index("group") == 1
+    mine = jnp.where(decoding, cache_values, cache_keys).T.reshape(count, width, cache_count)
+    meta = jnp.zeros((META, cache_count), jnp.int32)
+    meta = meta.at[0, :row_count].set(token_ids[0])
+    meta = meta.at[1].set(shard_lengths[0] // 16).at[2].set(shard_lengths[0] % 16)
+    meta = jnp.broadcast_to(meta.astype(jnp.bfloat16)[None], (count, META, cache_count))
+    packed = jnp.concatenate([mine, meta], 1)
+    kv, table = exchange(
+        packed, embed_table, norm_gain[None], query_weight, key_weight, value_weight
+    )
+    tokens = kv[:, :, width, :row_count].astype(jnp.int32).reshape(2, rows)
+    length = kv[0, :, width + 1 : width + 3, 0].astype(jnp.int32)
+    length = length[:, 0] * 16 + length[:, 1]
+    slot = jnp.arange(cache_count, dtype=jnp.int32)
+    bias = jnp.where(slot[None] < length[:, None], 0.0, -1e30).astype(jnp.float32)[:, None]
+    tables = table[:, :, :width]
+    query_table, key_table, value_table = tables[0], tables[1], tables[2]
+    key_tables = [key_table, partner(key_table), value_table]
+    span_tables = split_three(jnp.concatenate(key_tables, 1))
+    own_tables = split_three(
+        jnp.concatenate(key_tables + [query_table, partner(query_table)], 1)
+    )
+
+    def pick(tokens_in, tables_in):
+        hot = (tokens_in[:, None] == jnp.arange(3 * vocab, dtype=jnp.int32)[None] % vocab)
+        return jnp.dot(hot.astype(jnp.bfloat16), tables_in, preferred_element_type=jnp.float32)
+
+    index = jnp.arange(rows, dtype=jnp.int32)
+    span_cos, span_sin = rotation(span_offset[0] + index, width)
+    step_cos, step_sin = rotation(
+        span_offset[0] + rows + jnp.arange(8, dtype=jnp.int32) % STEPS, width
+    )
+    own_cos = jnp.where(decoding, jnp.tile(step_cos, (rows // 8, 1)), span_cos)
+    own_sin = jnp.where(decoding, jnp.tile(step_sin, (rows // 8, 1)), span_sin)
+    span = pick(tokens[0], span_tables)
+    own = pick(jnp.where(decoding, tokens[1], tokens[0]), own_tables)
+    span_key = (span[:, :width] * span_cos + span[:, width : 2 * width] * span_sin)
+    own_key = (own[:, :width] * own_cos + own[:, width : 2 * width] * own_sin)
+    query = own[:, 3 * width : 4 * width] * own_cos + own[:, 4 * width :] * own_sin
+    span_value = span[:, 2 * width :]
+    own_value = own[:, 2 * width : 3 * width]
+    out = attention(
+        query.astype(jnp.bfloat16),
+        own_key.astype(jnp.bfloat16),
+        own_value.astype(jnp.bfloat16),
+        span_key.astype(jnp.bfloat16),
+        span_value.astype(jnp.bfloat16),
+        kv,
+        bias,
+        row_count,
+    )
+    return give_back(out).reshape(local_width, row_count).T[None]
+
+
 def solution(mesh):
     placed = (
         P("group", "ctx"),
@@ -183,6 +564,8 @@
         P("ctx", "mp"),
         P("ctx", "mp"),
     )
+    heads = D // HD // mesh.shape["mp"]
+    body = by_heads if heads == 2 * mesh.shape["ctx"] else local
     return jax.shard_map(
-        local, mesh=mesh, in_specs=placed, out_specs=P("group", "ctx", "mp"), check_vma=False
-    )
+        body, mesh=mesh, in_specs=placed, out_specs=P("group", "ctx", "mp"), check_vma=False
+    )

time: 384 us -> 111 us (0.29)
  waiting for transfers between devices: 196 us -> 0 us
  Pallas kernels: 0 us -> 73.9 us
  matrix products: 53.2 us -> 2.13 us
  local copies, waits for them, and re-layouts: 57.1 us -> 19.4 us
  other arithmetic: 38.9 us -> 13.3 us
  starting transfers between devices: 17 us -> 0 us
  between operations: 14.2 us -> 1.61 us
  blocking collectives: 5.9 us -> 0 us
    all_to_all x3 -> x0, waiting for transfers between devices: 96.5 us -> none  [the longest x1 92.9 us: local(): lax.all_to_all(sums[None], 'ctx', split_axis=1, concat_axis=0, tiled=True)]
    pallas_call x0 -> x3, Pallas kernels: none -> 73.9 us  [the longest x1 30 us: attention(): pl.pallas_call(attention_kernel, grid=(blocks,), out_shape=jax.ShapeDtype...]
    reduce_scatter x3 -> x0, waiting for transfers between devices: 52 us -> none  [the longest x1 24.2 us: local(): lax.psum_scatter(query_part, 'mp', scatter_dimension=1, tiled=True)]
    dot_general x10 -> x2, matrix products: 53.2 us -> 2.13 us  [pick(): jnp.dot(hot.astype(jnp.bfloat16), tables_in, preferred_element_type=jnp.f...]
    all_gather x1 -> x0, waiting for transfers between devices: 46.9 us -> none  [local(): gathered = lax.all_gather(queries, 'ctx', axis=0, tiled=True)]
    reduce_sum x4 -> x0, other arithmetic: 19.5 us -> none  [the longest x2 18.5 us: block_partial(): block_sum = jnp.sum(weights, -1)]
    all_to_all x3 -> x0, starting transfers between devices: 13 us -> none  [the longest x1 6.07 us: local(): lax.all_to_all(sums[None], 'ctx', split_axis=1, concat_axis=0, tiled=True)]
    another operation x3 -> x4, local copies, waits for them, and re-layouts: 10.6 us -> 0.02 us  [the longest x2 0.02 us: partner(): pieces = table.reshape(table.shape[0], -1, 2, 2, HD // 4)]
  transfers between devices with their start and end apart: 9 -> 0, of which waited for: 7 -> 0; matrix products, arithmetic and copies ran while one was open for 16% -> 0% of each run, Pallas kernels for 0% -> 0%
where the time goes in v1:
time: 111 us; the launch traced here: 110 us
  Pallas kernels  73.9 us (67%)
  local copies, waits for them, and re-layouts  19.4 us (17%)
  other arithmetic  13.3 us (12%)
  matrix products  2.13 us (2%)
  between operations  1.61 us (1%)
    pallas_call x1, Pallas kernels, attention(): pl.pallas_call(attention_kernel, grid=(blocks,), out_shape=jax.ShapeDtype...  30 us
    pallas_call x1, Pallas kernels, exchange(): pl.pallas_call(exchange_kernel, out_shape=(jax.ShapeDtypeStruct((2,) + pa...  27.1 us
    pallas_call x1, Pallas kernels, give_back(): pl.pallas_call(give_back_kernel, out_shape=jax.ShapeDtypeStruct(parts.sha...  16.8 us
    unnamed x8, local copies, waits for them, and re-layouts  11.3 us
    convert_element_type x1, other arithmetic, by_heads(): own_key.astype(jnp.bfloat16)  8.14 us

profile of v1, /device:TPU:0, one launch (start us, length us, event | category | flops | bytes accessed | tf_op | source)
XLA Modules:
  0.0 110.4 jit_solution(68844267973828323)
XLA Ops:
  1.4 1.3 %broadcast_in_dim.86.gain = bf16[1,1280]{1,0:T(2,128)(2,1)} reshape(bf16[1280]{0:T(1024)(128)(2,1)} %param.20) | data formatting | bytes 5120 | tf_op jit(solution)/shard_map/broadcast_in_dim | solution.py:508
  2.7 0.1 fusion.23
  2.8 0.7 scatter.10
  3.5 0.1 scatter.14
  3.6 1.3 %select_bitcast_fusion = bf16[1280,384]{0,1:T(8,128)(2,1)S(1)} fusion(bf16[384,1280]{1,0:T(8,128)(2,1)} %param.25, bf16[384,1280]{1,0:T(8,128)(2,1)} %param.24, pred[]{:T(512)S(6)} %eq.44), kind=kLoop, calls=%fused_computation.13 | loop fusion | flops 491520 | bytes 2949121 | tf_op jit(solution)/shard_map/transpose | solution.py:501
  5.0 0.7 copy.38
  5.6 1.1 %pad_maximum_fusion.packed = bf16[8,176,384]{2,1,0:T(8,128)(2,1)} fusion(bf16[8,16,384]{2,1,0:T(8,128)(2,1)S(1)} %broadcast_in_dim.62, bf16[8,160,384]{2,1,0:T(8,128)(2,1)S(1)} %bitcast.46), kind=kLoop, calls=%fused_computation.4 | loop fusion | flops 2162688 | bytes 2162688 | tf_op jit(solution)/shard_map/concatenate | solution.py:506
  6.7 27.1 %exchange.1 = (bf16[2,8,176,384]{3,2,1,0:T(8,128)(2,1)}, f32[3,128,256]{2,1,0:T(8,128)}) custom-call(bf16[8,176,384]{2,1,0:T(8,128)(2,1)} %pad_maximum_fusion.packed, bf16[128,1280]{1,0:T(8,128)(2,1)} %embed.1, bf16[1,1280]{1,0:T(2,128)(2,1)} %broadcast_in_dim.86.gain, bf16[1280,2560]{1,0:T(8,128)(2,1)} %wq.1, bf16[1280,2560]{1,0:T(8,128)(2,1)} %wk.1, ...), custom_call_target="tpu_custom_call" | custom-call | tf_op jit(solution)/shard_map/exchange/pallas_call | solution.py:296
  33.8 0.7 slice_convert_fusion.3
  34.6 0.1 copy.52
  34.7 0.8 slice_convert_fusion.2
  35.5 0.7 compare_select_fusion.bias
  36.1 1.1 fusion.45
  37.2 0.1 copy.40
  37.4 0.1 copy.42
  37.5 0.1 copy.39
  37.7 0.1 copy.41
  37.8 0.2 concatenate.24
  38.0 0.2 reduce-precision_convert_fusion.3
  38.1 0.1 reduce-precision_convert_fusion.1
  38.2 0.9 fusion
  39.2 0.1 fusion.44
  39.3 1.0 copy.61.span_value
  40.4 0.3 copy.59
  40.7 0.3 copy.60
  41.1 1.2 %fusion.2 = f32[1024,800]{0,1:T(8,128)S(1)} fusion(s32[384]{0:T(512)S(1)} %add_select_fusion.2, s32[1024]{0:T(1024)S(1)} %broadcast_select_fusion, bf16[128,800]{1,0:T(8,128)(2,1)S(1)} %get-tuple-element.52, bf16[128,800]{1,0:T(8,128)(2,1)S(1)} %get-tuple-element.53, bf16[128,800]{1,0:T(8,128)(2,1)S(1)} %get-tuple-element.51), kind=kOutput, calls=%fused_computation.2 | convolution fusion | flops 631382016 | bytes 3896832 | tf_op jit(solution)/shard_map/dot_general | solution.py:525
  42.3 1.6 %fusion.43 = (f32[1024,160]{0,1:T(8,128)}, f32[1024,160]{0,1:T(8,128)}, f32[1024,160]{0,1:T(8,128)}, f32[1024,160]{0,1:T(8,128)}) fusion(f32[1024,800]{0,1:T(8,128)S(1)} %fusion.2), kind=kLoop, calls=%fused_computation.93 | loop fusion | bytes 5242880 | tf_op jit(solution)/shard_map/slice | solution.py:537
  43.9 1.0 copy.58.own_value
  44.9 1.4 %copy.56 = f32[1024,160]{1,0:T(8,128)S(1)} copy(f32[1024,160]{0,1:T(8,128)} %get-tuple-element.45) | data formatting | bytes 1310720
  46.3 2.4 %copy.55 = f32[1024,160]{1,0:T(8,128)} copy(f32[1024,160]{0,1:T(8,128)} %get-tuple-element.46) | data formatting | bytes 1310720
  48.7 2.4 %copy.54 = f32[1024,160]{1,0:T(8,128)} copy(f32[1024,160]{0,1:T(8,128)} %get-tuple-element.47) | data formatting | bytes 1310720
  51.1 2.4 %copy.57 = f32[1024,160]{1,0:T(8,128)} copy(f32[1024,160]{0,1:T(8,128)} %get-tuple-element.48) | data formatting | bytes 1310720
  53.5 8.1 %add_convert_fusion.1 = (bf16[1024,160]{1,0:T(8,128)(2,1)}, bf16[1024,160]{1,0:T(8,128)(2,1)}, bf16[1024,160]{1,0:T(8,128)(2,1)}) fusion(f32[1024,160]{1,0:T(8,128)} %copy.57, f32[1024,160]{1,0:T(8,128)S(1)} %copy.56, f32[8,160]{1,0:T(8,128)S(1)} %get-tuple-element.72, f32[160]{0:T(256)S(1)} %fusion.37, f32[1024]{0:T(1024)S(1)} %get-tuple-element.74, ...), kind=kLoop, calls=%fused_computation.8 | loop fusion | flops 2621440 | bytes 4934433 | tf_op jit(solution)/shard_map/convert_element_type | solution.py:543
  61.7 30.0 %attention.1.parts = bf16[8,160,128]{2,1,0:T(8,128)(2,1)} custom-call(bf16[1024,160]{1,0:T(8,128)(2,1)} %get-tuple-element.67.query, bf16[1024,160]{1,0:T(8,128)(2,1)} %get-tuple-element.66.own_key, bf16[1024,160]{1,0:T(8,128)(2,1)} %copy.58.own_value, bf16[1024,160]{1,0:T(8,128)(2,1)} %get-tuple-element.68.span_key, bf16[1024,160]{1,0:T(8,128)(2,1)} %copy.61.span_value, ...), custom_call_target="tpu_custom_call" | custom-call | tf_op jit(solution)/shard_map/attention/pallas_call | solution.py:391
  91.7 16.8 %give_back.1 = bf16[8,160,128]{2,1,0:T(8,128)(2,1)} custom-call(bf16[8,160,128]{2,1,0:T(8,128)(2,1)} %attention.1.parts), custom_call_target="tpu_custom_call" | custom-call | tf_op jit(solution)/shard_map/give_back/pallas_call | solution.py:444
  108.5 1.9 %copy.53 = bf16[1280,128]{0,1:T(8,128)(2,1)} copy(bf16[1280,128]{1,0:T(8,128)(2,1)} %bitcast.47) | data formatting | bytes 655360 | tf_op jit(solution)/shard_map/reshape | solution.py:551
  (23 shorter events, 0.3 us)

commit v2 on v0

--- a/solution.py
+++ b/solution.py
@@ -3,6 +3,8 @@
 import jax
 import jax.numpy as jnp
 from jax import lax
+from jax.experimental import pallas as pl
+from jax.experimental.pallas import tpu as pltpu
 from jax.sharding import PartitionSpec as P
 
 D = 2560
@@ -170,6 +172,454 @@
     return output.astype(jnp.bfloat16)[None]
 
 
+MESH_ID = pl.DeviceIdType.MESH
+WINDOW = 256
+ROW_BLOCK = 256
+HIDDEN = -1e30
+
+
+def flipped(index, mask):
+    result = index
+    bit = 1
+    while bit <= mask:
+        if mask & bit:
+            result = result + bit * (1 - 2 * (index // bit % 2))
+        bit *= 2
+    return result
+
+
+def masked_weights(scores, top):
+    return jnp.exp2((scores - top) * (math.log2(math.e) / math.sqrt(HD)))
+
+
+def across(left, right):
+    return lax.dot_general(
+        left, right, (((1,), (1,)), ((), ())), preferred_element_type=jnp.float32
+    )
+
+
+def layer_kernel(
+    offset, packed, note, embed, gain, frequency, wq, wk, wv, got,
+    kv, notes, wbuf, ss_out, ss_in, part_out, part_in, table, cosine, sine, query, own_key,
+    own_value, span_key, span_value, first_max, first_sum, first_acc, scores, bias, out_parts,
+    wsem, own_sem, note_send, note_recv, send_sem, recv_sem, relay_send, relay_recv, mp_send,
+    mp_recv, out_send, out_recv, out_own,
+):
+    count, width, keep = packed.shape
+    row_count = note.shape[1]
+    rows = row_count * count
+    vocab = embed.shape[0]
+    group, ctx, mp = lax.axis_index("group"), lax.axis_index("ctx"), lax.axis_index("mp")
+    decoding = group == 1
+    half = wq.shape[1] // 2
+    first = pl.multiple_of(ctx * width // 128 * 128, 128)
+    far_first = sorted(range(1, count), key=lambda mask: -mask)
+    barrier = pltpu.get_barrier_semaphore()
+    for mask in far_first:
+        for side in (group, 1 - group):
+            pl.semaphore_signal(
+                barrier,
+                inc=1,
+                device_id={"ctx": flipped(ctx, mask), "group": side},
+                device_id_type=MESH_ID,
+            )
+    pl.semaphore_signal(barrier, inc=1, device_id={"group": 1 - group}, device_id_type=MESH_ID)
+    pl.semaphore_signal(barrier, inc=1, device_id={"mp": 1 - mp}, device_id_type=MESH_ID)
+    loads = []
+    for slot in range(6):
+        side = 1 - mp if slot < 3 else mp
+        weight = (wq, wk, wv)[slot % 3]
+        column = pl.multiple_of(side * half + first, 128)
+        loads.append(
+            pltpu.make_async_copy(
+                weight.at[:, pl.ds(column, WINDOW)], wbuf.at[slot], wsem.at[slot]
+            )
+        )
+        loads[-1].start()
+    mine = pltpu.make_async_copy(packed.at[ctx], kv.at[group, ctx], own_sem.at[0])
+    mine.start()
+    my_note = pltpu.make_async_copy(note, notes.at[group, ctx], own_sem.at[1])
+    my_note.start()
+    embedded = embed[...].astype(jnp.float32)
+    ss_out[...] = jnp.broadcast_to(jnp.sum(embedded * embedded, 1, keepdims=True), ss_out.shape)
+    pl.semaphore_wait(barrier, 2 * count)
+    squares = pltpu.make_async_remote_copy(
+        src_ref=ss_out,
+        dst_ref=ss_in,
+        send_sem=mp_send.at[0],
+        recv_sem=mp_recv.at[0],
+        device_id={"mp": 1 - mp},
+        device_id_type=MESH_ID,
+    )
+    squares.start()
+    note_copies = []
+    for mask in range(count):
+        for same in (True, False):
+            if mask == 0 and same:
+                continue
+            slot = 2 * mask + (0 if same else 1)
+            note_copies.append(
+                pltpu.make_async_remote_copy(
+                    src_ref=note,
+                    dst_ref=notes.at[group, ctx],
+                    send_sem=note_send.at[slot],
+                    recv_sem=note_recv.at[slot],
+                    device_id={
+                        "ctx": flipped(ctx, mask),
+                        "group": group if same else 1 - group,
+                    },
+                    device_id_type=MESH_ID,
+                )
+            )
+            note_copies[-1].start()
+    sends = {}
+    for mask in far_first:
+        target = flipped(ctx, mask)
+        sends[mask] = pltpu.make_async_remote_copy(
+            src_ref=packed.at[target],
+            dst_ref=kv.at[group, ctx],
+            send_sem=send_sem.at[mask],
+            recv_sem=recv_sem.at[mask],
+            device_id={"ctx": target},
+            device_id_type=MESH_ID,
+        )
+        sends[mask].start()
+    relays = [
+        pltpu.make_async_remote_copy(
+            src_ref=packed.at[ctx],
+            dst_ref=kv.at[group, ctx],
+            send_sem=relay_send.at[0],
+            recv_sem=relay_recv.at[0],
+            device_id={"group": 1 - group},
+            device_id_type=MESH_ID,
+        )
+    ]
+    relays[0].start()
+
+    def relay(mask):
+        source = flipped(ctx, mask)
+        sends[mask].wait_recv()
+        relays.append(
+            pltpu.make_async_remote_copy(
+                src_ref=kv.at[group, source],
+                dst_ref=kv.at[group, source],
+                send_sem=relay_send.at[mask],
+                recv_sem=relay_recv.at[mask],
+                device_id={"group": 1 - group},
+                device_id_type=MESH_ID,
+            )
+        )
+        relays[-1].start()
+
+    squares.wait()
+    square_sum = (ss_out[...] + ss_in[...])[:, :1]
+    normal = (
+        embedded * lax.rsqrt(square_sum / D + 1e-05) * gain[...].astype(jnp.float32)
+    ).astype(jnp.bfloat16)
+    for slot in range(3):
+        loads[slot].wait()
+        part_out[slot] = jnp.dot(normal, wbuf[slot], preferred_element_type=jnp.float32)
+    parts = pltpu.make_async_remote_copy(
+        src_ref=part_out,
+        dst_ref=part_in,
+        send_sem=mp_send.at[1],
+        recv_sem=mp_recv.at[1],
+        device_id={"mp": 1 - mp},
+        device_id_type=MESH_ID,
+    )
+    parts.start()
+    for slot in range(3):
+        loads[slot + 3].wait()
+        table[slot] = jnp.dot(normal, wbuf[slot + 3], preferred_element_type=jnp.float32)
+
+    @pl.loop(0, rows // row_count + 1)
+    def _(block):
+        index = lax.broadcasted_iota(jnp.int32, (row_count, width), 0)
+        lane = lax.broadcasted_iota(jnp.int32, (row_count, width), 1)
+        last = block == rows // row_count
+        at = pl.multiple_of(block * row_count, row_count)
+        position = offset[0] + at + jnp.where(last, index % STEPS, index)
+        second = lane % HD >= HD // 2
+        angle = jnp.where(second, position // PROT, position % PROT).astype(
+            jnp.float32
+        ) * frequency[...]
+        cosine[pl.ds(at, row_count)] = jnp.cos(angle)
+        sine[pl.ds(at, row_count)] = jnp.sin(angle)
+
+    my_note.wait()
+    for copy in note_copies:
+        copy.wait()
+    for source in range(count):
+        length = notes[0, source, 1:2, :]
+        for at in range(0, keep, 128):
+            slot = lax.broadcasted_iota(jnp.int32, (1, 128), 1) + at
+            bias[source : source + 1, at : at + 128] = jnp.where(slot < length, 0.0, HIDDEN)
+    parts.wait()
+    shift = lax.rem(WINDOW - (ctx * width - first), WINDOW)
+    lane = lax.broadcasted_iota(jnp.int32, (vocab, WINDOW), 1)
+    even = lane % (HD // 2) < HD // 4
+    tables = []
+    for slot in range(3):
+        whole = pltpu.roll(table[slot] + part_in[slot], shift, 1)
+        tables.append(whole)
+        if slot < 2:
+            tables.append(
+                jnp.where(
+                    even,
+                    -pltpu.roll(whole, WINDOW - HD // 4, 1),
+                    pltpu.roll(whole, HD // 4, 1),
+                )
+            )
+    splits = []
+    for whole in tables:
+        high = whole.astype(jnp.bfloat16)
+        rest = whole - high.astype(jnp.float32)
+        middle = rest.astype(jnp.bfloat16)
+        low = (rest - middle.astype(jnp.float32)).astype(jnp.bfloat16)
+        splits.append((high, middle, low))
+
+    def picked(hot, split):
+        total = None
+        for part in split:
+            term = jnp.dot(hot, part, preferred_element_type=jnp.float32)
+            total = term if total is None else total + term
+        return total[:, :width]
+
+    def hot_rows(token_line):
+        letter = lax.broadcasted_iota(jnp.int32, (vocab, row_count), 0)
+        hot = (letter == token_line).astype(jnp.float32)
+        return jnp.transpose(hot).astype(jnp.bfloat16)
+
+    value_table = splits[4][:1]
+    for block in range(count):
+        here = slice(block * row_count, (block + 1) * row_count)
+        cos, sin = cosine[here], sine[here]
+        step_cos, step_sin = cosine[rows:], sine[rows:]
+        hot = hot_rows(notes[0, block, 0:1, :])
+        span_key[here] = (
+            picked(hot, splits[2]) * cos + picked(hot, splits[3]) * sin
+        ).astype(jnp.bfloat16)
+        span_value[here] = picked(hot, value_table).astype(jnp.bfloat16)
+        own_cos = jnp.where(decoding, step_cos, cos)
+        own_sin = jnp.where(decoding, step_sin, sin)
+        hot = hot_rows(jnp.where(decoding, notes[1, block, 0:1, :], notes[0, block, 0:1, :]))
+        query[here] = (
+            picked(hot, splits[0]) * own_cos + picked(hot, splits[1]) * own_sin
+        ).astype(jnp.bfloat16)
+        own_key[here] = (
+            picked(hot, splits[2]) * own_cos + picked(hot, splits[3]) * own_sin
+        ).astype(jnp.bfloat16)
+        own_value[here] = picked(hot, value_table).astype(jnp.bfloat16)
+
+    heads = width // HD
+    head_lane = lax.broadcasted_iota(jnp.int32, (ROW_BLOCK, width), 1)
+    inside = [(head_lane >= head * HD) & (head_lane < (head + 1) * HD) for head in range(heads)]
+
+    def one_head(block_query, head):
+        return jnp.where(inside[head], block_query, jnp.zeros_like(block_query))
+
+    row = lax.broadcasted_iota(jnp.int32, (ROW_BLOCK, rows), 0)
+    col = lax.broadcasted_iota(jnp.int32, (ROW_BLOCK, rows), 1)
+    own_row = lax.broadcasted_iota(jnp.int32, (ROW_BLOCK, ROW_BLOCK), 0)
+    own_col = lax.broadcasted_iota(jnp.int32, (ROW_BLOCK, ROW_BLOCK), 1)
+    own_limit = jnp.where(decoding, own_row, -1)
+    own_seen = (own_row // STEPS == own_col // STEPS) & (own_col <= own_limit)
+    blocks = rows // ROW_BLOCK
+    pending = list(far_first)
+    for block in range(blocks):
+        here = slice(block * ROW_BLOCK, (block + 1) * ROW_BLOCK)
+        limit = jnp.where(decoding, rows, row + block * ROW_BLOCK)
+        tops, sums, accs = None, None, None
+        for head in range(heads):
+            head_query = one_head(query[here], head)
+            span_scores = jnp.where(col <= limit, across(head_query, span_key[...]), HIDDEN)
+            own_scores = jnp.where(own_seen, across(head_query, own_key[here]), HIDDEN)
+            top = jnp.maximum(
+                jnp.max(span_scores, 1, keepdims=True), jnp.max(own_scores, 1, keepdims=True)
+            )
+            span_weights = masked_weights(span_scores, top)
+            own_weights = masked_weights(own_scores, top)
+            total = jnp.sum(span_weights, 1, keepdims=True) + jnp.sum(
+                own_weights, 1, keepdims=True
+            )
+            acc = jnp.dot(
+                span_weights.astype(jnp.bfloat16), span_value[...],
+                preferred_element_type=jnp.float32,
+            ) + jnp.dot(
+                own_weights.astype(jnp.bfloat16), own_value[here],
+                preferred_element_type=jnp.float32,
+            )
+            if head == 0:
+                tops, sums, accs = top, total, acc
+            else:
+                tops = jnp.where(inside[head], top, tops)
+                sums = jnp.where(inside[head], total, sums)
+                accs = jnp.where(inside[head], acc, accs)
+        first_max[here], first_sum[here], first_acc[here] = tops, sums, accs
+        for _ in range(-(-(count - 1) // blocks)):
+            if pending:
+                relay(pending.pop(0))
+    mine.wait()
+    for copy in relays:
+        copy.wait()
+    for mask in far_first:
+        sends[mask].wait_send()
+
+    per_block = ROW_BLOCK // row_count
+
+    def out_copy(owner):
+        return pltpu.make_async_remote_copy(
+            src_ref=out_parts.at[owner],
+            dst_ref=got.at[ctx],
+            send_sem=out_send.at[owner],
+            recv_sem=out_recv.at[ctx],
+            device_id={"ctx": owner},
+            device_id_type=MESH_ID,
+        )
+
+    @pl.loop(0, blocks)
+    def _(turn):
+        block = lax.rem(ctx // per_block + 1 + turn, blocks)
+        at = pl.multiple_of(block * ROW_BLOCK, ROW_BLOCK)
+        here = pl.ds(at, ROW_BLOCK)
+        block_query = query[here, :]
+        old_top, old_sum, old_acc = first_max[here, :], first_sum[here, :], first_acc[here, :]
+        result = None
+        for head in range(heads):
+            head_query = one_head(block_query, head)
+            for source in range(count):
+                part = jnp.dot(head_query, kv[0, source], preferred_element_type=jnp.float32)
+                scores[:, source * keep : (source + 1) * keep] = part + bias[source : source + 1]
+            before = old_top[:, head * HD : head * HD + 1]
+            top = jnp.maximum(jnp.max(scores[...], 1, keepdims=True), before)
+            ratio = masked_weights(before, top)
+            total = old_sum[:, head * HD : head * HD + 1] * ratio
+            acc = old_acc * ratio
+            for source in range(count):
+                weights = masked_weights(scores[:, source * keep : (source + 1) * keep], top)
+                total += jnp.sum(weights, 1, keepdims=True)
+                acc += across(weights.astype(jnp.bfloat16), kv[1, source])
+            head_out = acc / total
+            result = head_out if head == 0 else jnp.where(inside[head], head_out, result)
+        padded = jnp.concatenate(
+            [result, jnp.zeros((ROW_BLOCK, -width % 128), jnp.float32)], 1
+        )
+        turned = jnp.transpose(padded)[:width].astype(jnp.bfloat16)
+        for piece in range(per_block):
+            owner = block * per_block + piece
+            out_parts[owner] = turned[:, piece * row_count : (piece + 1) * row_count]
+
+            @pl.when(owner != ctx)
+            def _():
+                out_copy(owner).start()
+
+            @pl.when(owner == ctx)
+            def _():
+                pltpu.make_async_copy(out_parts.at[ctx], got.at[ctx], out_own).start()
+
+    pltpu.make_async_copy(out_parts.at[ctx], got.at[ctx], out_own).wait()
+    for mask in far_first:
+        peer = flipped(ctx, mask)
+        arrival = pltpu.make_async_remote_copy(
+            src_ref=out_parts.at[peer],
+            dst_ref=got.at[peer],
+            send_sem=out_send.at[peer],
+            recv_sem=out_recv.at[peer],
+            device_id={"ctx": peer},
+            device_id_type=MESH_ID,
+        )
+        arrival.wait()
+
+
+def layer(offset, packed, note, embed, gain, frequency, wq, wk, wv):
+    count, width, keep = packed.shape
+    row_count = note.shape[1]
+    rows = row_count * count
+    vocab, features = embed.shape
+    vmem = pl.BlockSpec(memory_space=pltpu.VMEM)
+    anywhere = pl.BlockSpec(memory_space=pl.ANY)
+    wide, narrow = jnp.float32, jnp.bfloat16
+    dma = pltpu.SemaphoreType.DMA
+    return pl.pallas_call(
+        layer_kernel,
+        out_shape=jax.ShapeDtypeStruct((count, width, row_count), narrow),
+        in_specs=[pl.BlockSpec(memory_space=pltpu.SMEM), anywhere, vmem, vmem, vmem, vmem]
+        + [anywhere] * 3,
+        out_specs=vmem,
+        scratch_shapes=[
+            pltpu.VMEM((2, count, width, keep), narrow),
+            pltpu.VMEM((2, count) + note.shape, jnp.int32),
+            pltpu.VMEM((6, features, WINDOW), narrow),
+            pltpu.VMEM((vocab, 128), wide),
+            pltpu.VMEM((vocab, 128), wide),
+            pltpu.VMEM((3, vocab, WINDOW), wide),
+            pltpu.VMEM((3, vocab, WINDOW), wide),
+            pltpu.VMEM((3, vocab, WINDOW), wide),
+            pltpu.VMEM((rows + row_count, width), wide),
+            pltpu.VMEM((rows + row_count, width), wide),
+            pltpu.VMEM((rows, width), narrow),
+            pltpu.VMEM((rows, width), narrow),
+            pltpu.VMEM((rows, width), narrow),
+            pltpu.VMEM((rows, width), narrow),
+            pltpu.VMEM((rows, width), narrow),
+            pltpu.VMEM((rows, width), wide),
+            pltpu.VMEM((rows, width), wide),
+            pltpu.VMEM((rows, width), wide),
+            pltpu.VMEM((ROW_BLOCK, count * keep), wide),
+            pltpu.VMEM((count, keep), wide),
+            pltpu.VMEM((count, width, row_count), narrow),
+            dma((6,)),
+            dma((2,)),
+            dma((2 * count,)),
+            dma((2 * count,)),
+            dma((count,)),
+            dma((count,)),
+            dma((count,)),
+            dma((count,)),
+            dma((2,)),
+            dma((2,)),
+            dma((count,)),
+            dma((count,)),
+            dma,
+        ],
+        compiler_params=pltpu.CompilerParams(
+            collective_id=0, has_side_effects=True, vmem_limit_bytes=56 << 20
+        ),
+        name="layer",
+    )(offset, packed, note, embed, gain, frequency, wq, wk, wv)
+
+
+def by_heads(
+    token_ids,
+    span_offset,
+    shard_lengths,
+    embed_table,
+    norm_gain,
+    query_weight,
+    key_weight,
+    value_weight,
+    cache_keys,
+    cache_values,
+):
+    row_count = token_ids.shape[1]
+    count = lax.axis_size("ctx")
+    cache_count, local_width = cache_keys.shape
+    width = local_width // count
+    decoding = lax.axis_index("group") == 1
+    packed = jnp.where(decoding, cache_values, cache_keys).T.reshape(count, width, cache_count)
+    note = jnp.where(
+        jnp.arange(8, dtype=jnp.int32)[:, None] == 0, token_ids, shard_lengths[:, None]
+    )
+    quarter = HD // 4
+    frequency = 10000.0 ** (-jnp.arange(quarter, dtype=jnp.float32) / quarter)
+    frequency = jnp.tile(frequency, width // quarter)[None]
+    out = layer(
+        span_offset, packed, note, embed_table, norm_gain[None], frequency,
+        query_weight, key_weight, value_weight,
+    )
+    return out.reshape(local_width, row_count).T[None]
+
+
 def solution(mesh):
     placed = (
         P("group", "ctx"),
@@ -183,6 +633,10 @@
         P("ctx", "mp"),
         P("ctx", "mp"),
     )
+    heads = D // HD // mesh.shape["mp"]
+    count = mesh.shape["ctx"]
+    fits = heads == 2 * count and count & (count - 1) == 0
+    body = by_heads if fits else local
     return jax.shard_map(
-        local, mesh=mesh, in_specs=placed, out_specs=P("group", "ctx", "mp"), check_vma=False
-    )
+        body, mesh=mesh, in_specs=placed, out_specs=P("group", "ctx", "mp"), check_vma=False
+    )

time: 384 us -> 66.1 us (0.17)
  waiting for transfers between devices: 196 us -> 0 us
  Pallas kernels: 0 us -> 56.7 us
  matrix products: 53.2 us -> 0 us
  local copies, waits for them, and re-layouts: 57.1 us -> 5.11 us
  other arithmetic: 38.9 us -> 2.64 us
  starting transfers between devices: 17 us -> 0 us
  between operations: 14.2 us -> 1.32 us
  blocking collectives: 5.9 us -> 0 us
    all_to_all x3 -> x0, waiting for transfers between devices: 96.5 us -> none  [the longest x1 92.9 us: local(): lax.all_to_all(sums[None], 'ctx', split_axis=1, concat_axis=0, tiled=True)]
    pallas_call x0 -> x1, Pallas kernels: none -> 56.7 us  [layer(): pl.pallas_call(layer_kernel, out_shape=jax.ShapeDtypeStruct((count, width...]
    dot_general x10 -> x0, matrix products: 53.2 us -> none  [the longest x2 18.3 us: block_partial(): jnp.einsum('hqk,khd->qhd', weights.astype(jnp.bfloat16), value_heads, pre...]
    reduce_scatter x3 -> x0, waiting for transfers between devices: 52 us -> none  [the longest x1 24.2 us: local(): lax.psum_scatter(query_part, 'mp', scatter_dimension=1, tiled=True)]
    all_gather x1 -> x0, waiting for transfers between devices: 46.9 us -> none  [local(): gathered = lax.all_gather(queries, 'ctx', axis=0, tiled=True)]
    reduce_sum x4 -> x0, other arithmetic: 19.5 us -> none  [the longest x2 18.5 us: block_partial(): block_sum = jnp.sum(weights, -1)]
    all_to_all x3 -> x0, starting transfers between devices: 13 us -> none  [the longest x1 6.07 us: local(): lax.all_to_all(sums[None], 'ctx', split_axis=1, concat_axis=0, tiled=True)]
    unnamed x22 -> x0, local copies, waits for them, and re-layouts: 11.9 us -> none
  transfers between devices with their start and end apart: 9 -> 0, of which waited for: 7 -> 0; matrix products, arithmetic and copies ran while one was open for 16% -> 0% of each run, Pallas kernels for 0% -> 0%
where the time goes in v2:
time: 66.1 us; the launch traced here: 65.8 us
  Pallas kernels  56.7 us (86%)
  local copies, waits for them, and re-layouts  5.11 us (8%)
  other arithmetic  2.64 us (4%)
  between operations  1.32 us (2%)
    pallas_call x1, Pallas kernels, layer(): pl.pallas_call(layer_kernel, out_shape=jax.ShapeDtypeStruct((count, width...  56.7 us
    reshape x1, local copies, waits for them, and re-layouts, by_heads(): return out.reshape(local_width, row_count).T[None]  1.87 us
    transpose x1, local copies, waits for them, and re-layouts, by_heads(): jnp.where(decoding, cache_values, cache_keys)  1.33 us

profile of v2, /device:TPU:0, one launch (start us, length us, event | category | flops | bytes accessed | tf_op | source)
XLA Modules:
  0.0 65.8 jit_solution(17435404397878463331)
XLA Ops:
  0.0 1.3 %select_bitcast_fusion = bf16[1280,384]{0,1:T(8,128)(2,1)S(1)} fusion(bf16[384,1280]{1,0:T(8,128)(2,1)} %param.19, bf16[384,1280]{1,0:T(8,128)(2,1)} %param.18, pred[]{:T(512)S(6)} %eq.11), kind=kLoop, calls=%fused_computation | loop fusion | flops 491520 | bytes 2949121 | tf_op jit(solution)/shard_map/transpose | solution.py:609
  1.3 1.3 %copy.11 = bf16[1280,384]{1,0:T(8,128)(2,1)} copy(bf16[1280,384]{0,1:T(8,128)(2,1)S(1)} %select_bitcast_fusion) | data formatting | bytes 1966080 | tf_op jit(solution)/shard_map/transpose | solution.py:609
  2.7 0.6 broadcast_in_dim_tile.3.frequency
  3.3 1.3 %broadcast_in_dim.41.gain = bf16[1,1280]{1,0:T(2,128)(2,1)} reshape(bf16[1280]{0:T(1024)(128)(2,1)} %param.14) | data formatting | bytes 5120 | tf_op jit(solution)/shard_map/broadcast_in_dim | solution.py:617
  5.2 1.3 %broadcast_select_fusion.note = s32[8,128]{1,0:T(8,128)} fusion(s32[]{:T(128)} %bitcast.9, s32[128]{0:T(128)} %bitcast.12, pred[8]{0:T(512)(128)(4,1)S(1)} %iota_compare_fusion), kind=kLoop, calls=%fused_computation.1 | loop fusion | flops 1024 | bytes 4620 | tf_op jit(solution)/shard_map/jit(_where)/select_n | solution.py:610
  7.2 56.7 %layer.1 = bf16[8,160,128]{2,1,0:T(8,128)(2,1)} custom-call(s32[1]{0:T(128)S(6)} %copy.13.offset, bf16[8,160,384]{2,1,0:T(8,128)(2,1)} %bitcast.10, s32[8,128]{1,0:T(8,128)} %broadcast_select_fusion.note, bf16[128,1280]{1,0:T(8,128)(2,1)} %embed.1, bf16[1,1280]{1,0:T(2,128)(2,1)} %broadcast_in_dim.41.gain, f32[1,160]{1,0:T(1,128)} %broadcast_in_dim_tile.3.frequency, ...), custom_call_target="tpu_custom_call" | custom-call | tf_op jit(solution)/shard_map/layer/pallas_call | solution.py:543
  63.9 1.9 %copy.12 = bf16[1280,128]{0,1:T(8,128)(2,1)} copy(bf16[1280,128]{1,0:T(8,128)(2,1)} %bitcast.11) | data formatting | bytes 655360 | tf_op jit(solution)/shard_map/reshape | solution.py:620
  (3 shorter events, 0.0 us)

commit v3 on v2

--- a/solution.py
+++ b/solution.py
@@ -2,6 +2,7 @@
 
 import jax
 import jax.numpy as jnp
+import numpy as np
 from jax import lax
 from jax.experimental import pallas as pl
 from jax.experimental.pallas import tpu as pltpu
@@ -174,7 +175,7 @@
 
 MESH_ID = pl.DeviceIdType.MESH
 WINDOW = 256
-ROW_BLOCK = 256
+ROW_BLOCK = 128
 HIDDEN = -1e30
 
 
@@ -199,8 +200,8 @@
 
 
 def layer_kernel(
-    offset, packed, note, embed, gain, frequency, wq, wk, wv, got,
-    kv, notes, wbuf, ss_out, ss_in, part_out, part_in, table, cosine, sine, query, own_key,
+    offset, length_here, packed, token_line, embed, gain, frequency, wq, wk, wv, got,
+    kv, note, notes, wbuf, ss_out, ss_in, part_out, part_in, table, cosine, sine, query, own_key,
     own_value, span_key, span_value, first_max, first_sum, first_acc, scores, bias, out_parts,
     wsem, own_sem, note_send, note_recv, send_sem, recv_sem, relay_send, relay_recv, mp_send,
     mp_recv, out_send, out_recv, out_own,
@@ -213,9 +214,11 @@
     decoding = group == 1
     half = wq.shape[1] // 2
     first = pl.multiple_of(ctx * width // 128 * 128, 128)
-    far_first = sorted(range(1, count), key=lambda mask: -mask)
+    near_first = sorted(range(1, count), key=lambda mask: mask)
+    note_line = lax.broadcasted_iota(jnp.int32, note.shape, 0)
+    note[...] = jnp.where(note_line == 0, token_line[...], length_here[0])
     barrier = pltpu.get_barrier_semaphore()
-    for mask in far_first:
+    for mask in near_first:
         for side in (group, 1 - group):
             pl.semaphore_signal(
                 barrier,
@@ -273,7 +276,7 @@
             )
             note_copies[-1].start()
     sends = {}
-    for mask in far_first:
+    for mask in near_first:
         target = flipped(ctx, mask)
         sends[mask] = pltpu.make_async_remote_copy(
             src_ref=packed.at[target],
@@ -314,7 +317,7 @@
     squares.wait()
     square_sum = (ss_out[...] + ss_in[...])[:, :1]
     normal = (
-        embedded * lax.rsqrt(square_sum / D + 1e-05) * gain[...].astype(jnp.float32)
+        embedded * lax.rsqrt(square_sum / D + 1e-05) * gain[...].astype(jnp.float32)[None]
     ).astype(jnp.bfloat16)
     for slot in range(3):
         loads[slot].wait()
@@ -332,19 +335,24 @@
         loads[slot + 3].wait()
         table[slot] = jnp.dot(normal, wbuf[slot + 3], preferred_element_type=jnp.float32)
 
-    @pl.loop(0, rows // row_count + 1)
-    def _(block):
-        index = lax.broadcasted_iota(jnp.int32, (row_count, width), 0)
-        lane = lax.broadcasted_iota(jnp.int32, (row_count, width), 1)
-        last = block == rows // row_count
-        at = pl.multiple_of(block * row_count, row_count)
-        position = offset[0] + at + jnp.where(last, index % STEPS, index)
-        second = lane % HD >= HD // 2
-        angle = jnp.where(second, position // PROT, position % PROT).astype(
-            jnp.float32
-        ) * frequency[...]
-        cosine[pl.ds(at, row_count)] = jnp.cos(angle)
-        sine[pl.ds(at, row_count)] = jnp.sin(angle)
+    def turn(at, size, column, homolog, lane):
+        angle = jnp.where(lane % HD >= HD // 2, homolog, column).astype(jnp.float32)
+        angle = angle * frequency[...]
+        cosine[pl.ds(at, size)] = jnp.cos(angle)
+        sine[pl.ds(at, size)] = jnp.sin(angle)
+
+    small = lax.broadcasted_iota(jnp.int32, (8, width), 0)
+    small_lane = lax.broadcasted_iota(jnp.int32, (8, width), 1)
+    homolog = offset[0] // PROT + small
+    turn(PROT, 8, homolog, homolog, small_lane)
+    position = offset[0] + rows + small % STEPS
+    turn(PROT + 8, 8, position % PROT, position // PROT, small_lane)
+
+    @pl.loop(0, PROT // 64)
+    def _(piece):
+        at = pl.multiple_of(piece * 64, 64)
+        column = (offset[0] + at + lax.broadcasted_iota(jnp.int32, (64, width), 0)) % PROT
+        turn(at, 64, column, column, lax.broadcasted_iota(jnp.int32, (64, width), 1))
 
     my_note.wait()
     for copy in note_copies:
@@ -370,44 +378,48 @@
                     pltpu.roll(whole, HD // 4, 1),
                 )
             )
-    splits = []
+    stacks = []
     for whole in tables:
         high = whole.astype(jnp.bfloat16)
-        rest = whole - high.astype(jnp.float32)
-        middle = rest.astype(jnp.bfloat16)
-        low = (rest - middle.astype(jnp.float32)).astype(jnp.bfloat16)
-        splits.append((high, middle, low))
-
-    def picked(hot, split):
-        total = None
-        for part in split:
-            term = jnp.dot(hot, part, preferred_element_type=jnp.float32)
-            total = term if total is None else total + term
-        return total[:, :width]
-
-    def hot_rows(token_line):
+        rest = (whole - high.astype(jnp.float32)).astype(jnp.bfloat16)
+        stacks.append(jnp.concatenate([high, rest], 0))
+    value_table = tables[4].astype(jnp.bfloat16)
+
+    def picked(hot, table_in):
+        return jnp.dot(hot, table_in, preferred_element_type=jnp.float32)[:, :width]
+
+    def hot_rows(lines):
         letter = lax.broadcasted_iota(jnp.int32, (vocab, row_count), 0)
-        hot = (letter == token_line).astype(jnp.float32)
-        return jnp.transpose(hot).astype(jnp.bfloat16)
-
-    value_table = splits[4][:1]
-    for block in range(count):
-        here = slice(block * row_count, (block + 1) * row_count)
-        cos, sin = cosine[here], sine[here]
-        step_cos, step_sin = cosine[rows:], sine[rows:]
-        hot = hot_rows(notes[0, block, 0:1, :])
+        hots = [jnp.transpose((letter == line).astype(jnp.float32)) for line in lines]
+        return jnp.concatenate(hots, 0).astype(jnp.bfloat16)
+
+    turn_row = lax.broadcasted_iota(jnp.int32, (PROT, width), 0)
+    turn_second = lax.broadcasted_iota(jnp.int32, (PROT, width), 1) % HD >= HD // 2
+    wrapped = offset[0] % PROT + turn_row >= PROT
+    lines_per = PROT // row_count
+    for block in range(rows // PROT):
+        here = slice(block * PROT, (block + 1) * PROT)
+        lines = range(block * lines_per, (block + 1) * lines_per)
+        span_turn, own_turn = [], []
+        for angles in (cosine, sine):
+            low = PROT + block
+            homolog_part = jnp.where(wrapped, angles[low + 1 : low + 2], angles[low : low + 1])
+            span_turn.append(jnp.where(turn_second, homolog_part, angles[:PROT]))
+            steps = jnp.concatenate([angles[PROT + 8 : PROT + 16]] * (PROT // 8), 0)
+            own_turn.append(jnp.where(decoding, steps, span_turn[-1]))
+        hot = hot_rows([notes[0, line, 0:1, :] for line in lines])
+        twice = jnp.concatenate([hot, hot], 1)
         span_key[here] = (
-            picked(hot, splits[2]) * cos + picked(hot, splits[3]) * sin
+            picked(twice, stacks[2]) * span_turn[0] + picked(twice, stacks[3]) * span_turn[1]
         ).astype(jnp.bfloat16)
         span_value[here] = picked(hot, value_table).astype(jnp.bfloat16)
-        own_cos = jnp.where(decoding, step_cos, cos)
-        own_sin = jnp.where(decoding, step_sin, sin)
-        hot = hot_rows(jnp.where(decoding, notes[1, block, 0:1, :], notes[0, block, 0:1, :]))
+        hot = hot_rows([notes[group, line, 0:1, :] for line in lines])
+        twice = jnp.concatenate([hot, hot], 1)
         query[here] = (
-            picked(hot, splits[0]) * own_cos + picked(hot, splits[1]) * own_sin
+            picked(twice, stacks[0]) * own_turn[0] + picked(twice, stacks[1]) * own_turn[1]
         ).astype(jnp.bfloat16)
         own_key[here] = (
-            picked(hot, splits[2]) * own_cos + picked(hot, splits[3]) * own_sin
+            picked(twice, stacks[2]) * own_turn[0] + picked(twice, stacks[3]) * own_turn[1]
         ).astype(jnp.bfloat16)
         own_value[here] = picked(hot, value_table).astype(jnp.bfloat16)
 
@@ -425,7 +437,7 @@
     own_limit = jnp.where(decoding, own_row, -1)
     own_seen = (own_row // STEPS == own_col // STEPS) & (own_col <= own_limit)
     blocks = rows // ROW_BLOCK
-    pending = list(far_first)
+    pending = list(near_first)
     for block in range(blocks):
         here = slice(block * ROW_BLOCK, (block + 1) * ROW_BLOCK)
         limit = jnp.where(decoding, rows, row + block * ROW_BLOCK)
@@ -462,7 +474,7 @@
     mine.wait()
     for copy in relays:
         copy.wait()
-    for mask in far_first:
+    for mask in near_first:
         sends[mask].wait_send()
 
     per_block = ROW_BLOCK // row_count
@@ -518,7 +530,7 @@
                 pltpu.make_async_copy(out_parts.at[ctx], got.at[ctx], out_own).start()
 
     pltpu.make_async_copy(out_parts.at[ctx], got.at[ctx], out_own).wait()
-    for mask in far_first:
+    for mask in near_first:
         peer = flipped(ctx, mask)
         arrival = pltpu.make_async_remote_copy(
             src_ref=out_parts.at[peer],
@@ -531,9 +543,9 @@
         arrival.wait()
 
 
-def layer(offset, packed, note, embed, gain, frequency, wq, wk, wv):
+def layer(offset, length_here, packed, token_line, embed, gain, frequency, wq, wk, wv):
     count, width, keep = packed.shape
-    row_count = note.shape[1]
+    row_count = token_line.shape[1]
     rows = row_count * count
     vocab, features = embed.shape
     vmem = pl.BlockSpec(memory_space=pltpu.VMEM)
@@ -543,20 +555,21 @@
     return pl.pallas_call(
         layer_kernel,
         out_shape=jax.ShapeDtypeStruct((count, width, row_count), narrow),
-        in_specs=[pl.BlockSpec(memory_space=pltpu.SMEM), anywhere, vmem, vmem, vmem, vmem]
+        in_specs=[pl.BlockSpec(memory_space=pltpu.SMEM)] * 2 + [anywhere] + [vmem] * 4
         + [anywhere] * 3,
         out_specs=vmem,
         scratch_shapes=[
             pltpu.VMEM((2, count, width, keep), narrow),
-            pltpu.VMEM((2, count) + note.shape, jnp.int32),
+            pltpu.VMEM((8, row_count), jnp.int32),
+            pltpu.VMEM((2, count, 8, row_count), jnp.int32),
             pltpu.VMEM((6, features, WINDOW), narrow),
             pltpu.VMEM((vocab, 128), wide),
             pltpu.VMEM((vocab, 128), wide),
             pltpu.VMEM((3, vocab, WINDOW), wide),
             pltpu.VMEM((3, vocab, WINDOW), wide),
             pltpu.VMEM((3, vocab, WINDOW), wide),
-            pltpu.VMEM((rows + row_count, width), wide),
-            pltpu.VMEM((rows + row_count, width), wide),
+            pltpu.VMEM((PROT + 16, width), wide),
+            pltpu.VMEM((PROT + 16, width), wide),
             pltpu.VMEM((rows, width), narrow),
             pltpu.VMEM((rows, width), narrow),
             pltpu.VMEM((rows, width), narrow),
@@ -586,7 +599,7 @@
             collective_id=0, has_side_effects=True, vmem_limit_bytes=56 << 20
         ),
         name="layer",
-    )(offset, packed, note, embed, gain, frequency, wq, wk, wv)
+    )(offset, length_here, packed, token_line, embed, gain, frequency, wq, wk, wv)
 
 
 def by_heads(
@@ -607,14 +620,11 @@
     width = local_width // count
     decoding = lax.axis_index("group") == 1
     packed = jnp.where(decoding, cache_values, cache_keys).T.reshape(count, width, cache_count)
-    note = jnp.where(
-        jnp.arange(8, dtype=jnp.int32)[:, None] == 0, token_ids, shard_lengths[:, None]
-    )
     quarter = HD // 4
-    frequency = 10000.0 ** (-jnp.arange(quarter, dtype=jnp.float32) / quarter)
-    frequency = jnp.tile(frequency, width // quarter)[None]
+    frequency = np.power(10000.0, -np.arange(quarter) / quarter).astype(np.float32)
+    frequency = jnp.asarray(np.tile(frequency, width // quarter)[None])
     out = layer(
-        span_offset, packed, note, embed_table, norm_gain[None], frequency,
+        span_offset, shard_lengths, packed, token_ids, embed_table, norm_gain, frequency,
         query_weight, key_weight, value_weight,
     )
     return out.reshape(local_width, row_count).T[None]
@@ -635,7 +645,7 @@
     )
     heads = D // HD // mesh.shape["mp"]
     count = mesh.shape["ctx"]
-    fits = heads == 2 * count and count & (count - 1) == 0
+    fits = heads == 2 * count and count == 8
     body = by_heads if fits else local
     return jax.shard_map(
         body, mesh=mesh, in_specs=placed, out_specs=P("group", "ctx", "mp"), check_vma=False

time: 66.1 us -> 56.7 us (0.86)
  Pallas kernels: 56.7 us -> 50.7 us
  local copies, waits for them, and re-layouts: 5.11 us -> 3.2 us
  other arithmetic: 2.64 us -> 1.31 us
    pallas_call x1, Pallas kernels: 56.7 us -> 50.7 us  [layer(): pl.pallas_call(layer_kernel, out_shape=jax.ShapeDtypeStruct((count, width...]
    select_n x1 -> x0, other arithmetic: 1.32 us -> none  [by_heads(): jnp.where(jnp.arange(8, dtype=jnp.int32)[:, None] == 0, token_ids, shard_...]
    broadcast_in_dim x1 -> x0, local copies, waits for them, and re-layouts: 1.28 us -> none  [by_heads(): norm_gain[None]]
where the time goes in v3:
time: 56.7 us; the launch traced here: 56.5 us
  Pallas kernels  50.7 us (89%)
  local copies, waits for them, and re-layouts  3.2 us (6%)
  other arithmetic  1.31 us (2%)
  between operations  1.31 us (2%)
    pallas_call x1, Pallas kernels, layer(): pl.pallas_call(layer_kernel, out_shape=jax.ShapeDtypeStruct((count, width...  50.7 us
    reshape x1, local copies, waits for them, and re-layouts, by_heads(): return out.reshape(local_width, row_count).T[None]  1.87 us
    transpose x1, local copies, waits for them, and re-layouts, by_heads(): jnp.where(decoding, cache_values, cache_keys)  1.33 us
    transpose x1, other arithmetic, by_heads(): jnp.where(decoding, cache_values, cache_keys)  1.31 us

profile of v3, /device:TPU:0, one launch (start us, length us, event | category | flops | bytes accessed | tf_op | source)
XLA Modules:
  0.0 56.5 jit_solution(17558768736206004263)
XLA Ops:
  0.0 1.3 %select_bitcast_fusion = bf16[1280,384]{0,1:T(8,128)(2,1)S(1)} fusion(bf16[384,1280]{1,0:T(8,128)(2,1)} %param.20, bf16[384,1280]{1,0:T(8,128)(2,1)} %param.19, pred[]{:T(512)S(6)} %eq.3), kind=kLoop, calls=%fused_computation | loop fusion | flops 491520 | bytes 2949121 | tf_op jit(solution)/shard_map/transpose | solution.py:622
  1.3 1.3 %copy.12 = bf16[1280,384]{1,0:T(8,128)(2,1)} copy(bf16[1280,384]{0,1:T(8,128)(2,1)S(1)} %select_bitcast_fusion) | data formatting | bytes 1966080 | tf_op jit(solution)/shard_map/transpose | solution.py:622
  3.9 50.7 %layer.1 = bf16[8,160,128]{2,1,0:T(8,128)(2,1)} custom-call(s32[1]{0:T(128)S(6)} %copy.14.offset, s32[1]{0:T(128)S(6)} %copy.15.length_here, bf16[8,160,384]{2,1,0:T(8,128)(2,1)} %bitcast.7, s32[1,128]{1,0:T(1,128)} %token_line.1, bf16[128,1280]{1,0:T(8,128)(2,1)} %embed.1, bf16[1280]{0:T(1024)(128)(2,1)} %gain.1, f32[1,160]{1,0:T(1,128)} %constant.10.clone.frequency, ...), custom_call_target="tpu_custom_call" | custom-call | tf_op jit(solution)/shard_map/layer/pallas_call | solution.py:555
  54.6 1.9 %copy.13 = bf16[1280,128]{0,1:T(8,128)(2,1)} copy(bf16[1280,128]{1,0:T(8,128)(2,1)} %bitcast.8) | data formatting | bytes 655360 | tf_op jit(solution)/shard_map/reshape | solution.py:630

commit v4 on v3

--- a/solution.py
+++ b/solution.py
@@ -319,18 +319,32 @@
     normal = (
         embedded * lax.rsqrt(square_sum / D + 1e-05) * gain[...].astype(jnp.float32)[None]
     ).astype(jnp.bfloat16)
+    mine_rows = pl.ds(pl.multiple_of(group * (vocab // 2), 8), vocab // 2)
+    parts, part_relays = [], []
     for slot in range(3):
         loads[slot].wait()
         part_out[slot] = jnp.dot(normal, wbuf[slot], preferred_element_type=jnp.float32)
-    parts = pltpu.make_async_remote_copy(
-        src_ref=part_out,
-        dst_ref=part_in,
-        send_sem=mp_send.at[1],
-        recv_sem=mp_recv.at[1],
-        device_id={"mp": 1 - mp},
-        device_id_type=MESH_ID,
-    )
-    parts.start()
+        parts.append(
+            pltpu.make_async_remote_copy(
+                src_ref=part_out.at[slot, mine_rows],
+                dst_ref=part_in.at[slot, mine_rows],
+                send_sem=mp_send.at[1 + slot],
+                recv_sem=mp_recv.at[1 + slot],
+                device_id={"mp": 1 - mp},
+                device_id_type=MESH_ID,
+            )
+        )
+        parts[-1].start()
+        part_relays.append(
+            pltpu.make_async_remote_copy(
+                src_ref=part_in.at[slot, mine_rows],
+                dst_ref=part_in.at[slot, mine_rows],
+                send_sem=mp_send.at[4 + slot],
+                recv_sem=mp_recv.at[4 + slot],
+                device_id={"group": 1 - group},
+                device_id_type=MESH_ID,
+            )
+        )
     for slot in range(3):
         loads[slot + 3].wait()
         table[slot] = jnp.dot(normal, wbuf[slot + 3], preferred_element_type=jnp.float32)
@@ -362,7 +376,11 @@
         for at in range(0, keep, 128):
             slot = lax.broadcasted_iota(jnp.int32, (1, 128), 1) + at
             bias[source : source + 1, at : at + 128] = jnp.where(slot < length, 0.0, HIDDEN)
-    parts.wait()
+    for slot in range(3):
+        parts[slot].wait()
+        part_relays[slot].start()
+    for copy in part_relays:
+        copy.wait()
     shift = lax.rem(WINDOW - (ctx * width - first), WINDOW)
     lane = lax.broadcasted_iota(jnp.int32, (vocab, WINDOW), 1)
     even = lane % (HD // 2) < HD // 4
@@ -589,8 +607,8 @@
             dma((count,)),
             dma((count,)),
             dma((count,)),
-            dma((2,)),
-            dma((2,)),
+            dma((7,)),
+            dma((7,)),
             dma((count,)),
             dma((count,)),
             dma,

time: 56.7 us -> 54.6 us (0.963)
  Pallas kernels: 50.7 us -> 48.5 us
    pallas_call x1, Pallas kernels: 50.7 us -> 48.5 us  [layer(): pl.pallas_call(layer_kernel, out_shape=jax.ShapeDtypeStruct((count, width...]
where the time goes in v4:
time: 54.6 us; the launch traced here: 54.3 us
  Pallas kernels  48.5 us (89%)
  local copies, waits for them, and re-layouts  3.2 us (6%)
  other arithmetic  1.31 us (2%)
  between operations  1.31 us (2%)
    pallas_call x1, Pallas kernels, layer(): pl.pallas_call(layer_kernel, out_shape=jax.ShapeDtypeStruct((count, width...  48.5 us
    reshape x1, local copies, waits for them, and re-layouts, by_heads(): return out.reshape(local_width, row_count).T[None]  1.87 us
    transpose x1, local copies, waits for them, and re-layouts, by_heads(): jnp.where(decoding, cache_values, cache_keys)  1.33 us
    transpose x1, other arithmetic, by_heads(): jnp.where(decoding, cache_values, cache_keys)  1.31 us

profile of v4, /device:TPU:0, one launch (start us, length us, event | category | flops | bytes accessed | tf_op | source)
XLA Modules:
  0.0 54.3 jit_solution(9596101795300577165)
XLA Ops:
  0.0 1.3 %select_bitcast_fusion = bf16[1280,384]{0,1:T(8,128)(2,1)S(1)} fusion(bf16[384,1280]{1,0:T(8,128)(2,1)} %param.20, bf16[384,1280]{1,0:T(8,128)(2,1)} %param.19, pred[]{:T(512)S(6)} %eq.3), kind=kLoop, calls=%fused_computation | loop fusion | flops 491520 | bytes 2949121 | tf_op jit(solution)/shard_map/transpose | solution.py:640
  1.3 1.3 %copy.12 = bf16[1280,384]{1,0:T(8,128)(2,1)} copy(bf16[1280,384]{0,1:T(8,128)(2,1)S(1)} %select_bitcast_fusion) | data formatting | bytes 1966080 | tf_op jit(solution)/shard_map/transpose | solution.py:640
  3.9 48.5 %layer.1 = bf16[8,160,128]{2,1,0:T(8,128)(2,1)} custom-call(s32[1]{0:T(128)S(6)} %copy.14.offset, s32[1]{0:T(128)S(6)} %copy.15.length_here, bf16[8,160,384]{2,1,0:T(8,128)(2,1)} %bitcast.7, s32[1,128]{1,0:T(1,128)} %token_line.1, bf16[128,1280]{1,0:T(8,128)(2,1)} %embed.1, bf16[1280]{0:T(1024)(128)(2,1)} %gain.1, f32[1,160]{1,0:T(1,128)} %constant.10.clone.frequency, ...), custom_call_target="tpu_custom_call" | custom-call | tf_op jit(solution)/shard_map/layer/pallas_call | solution.py:573
  52.4 1.9 %copy.13 = bf16[1280,128]{0,1:T(8,128)(2,1)} copy(bf16[1280,128]{1,0:T(8,128)(2,1)} %bitcast.8) | data formatting | bytes 655360 | tf_op jit(solution)/shard_map/reshape | solution.py:648
